TPU v7x, 256 devices: a whole 4x4x8 slice. The times are simulated.
256 devices in a mesh: col: 64 (over x, y, z_lo), slab: 4 (over z_hi, core).
Axes of the slice: x: 4, y: 4, z: 8 (z_hi: 2, z_lo: 4; z = z_hi * 4 + z_lo), core: 2. Of those that a mesh axis runs over, the one named last changes fastest.
Arguments:
- offsets: float32 [2, 128, 256, 128], P(None, 'col', 'slab'), may hold values from 0 to 1
- velocity: float32 [2, 128, 256, 128], P(None, 'col', 'slab'), may hold values from -8 to 8
- particle_mass: float32 [128, 256, 128], P('col', 'slab'), may hold values from 0.5 to 2
- pressure_start: float32 [128, 256, 128], P('col', 'slab'), may hold values from -4 to 4
- counts: int32 [128, 256], P('col', 'slab'), may hold values from 1 to 128
- leaving_slot: int32 [512, 4, 128], P('col', 'slab'), may hold values from 0 to 16383
- leaving_count: int32 [512, 4], P('col', 'slab'), may hold values from 1 to 128
- leaving_side: int32 [512, 4], P('col', 'slab'), may hold values from 0 to 1
Outputs:
- density_ratio: float32 [128, 256, 128], P('col', 'slab')
- pressure: float32 [128, 256, 128], P('col', 'slab')
- acceleration: float32 [2, 128, 256, 128], P(None, 'col', 'slab')
- velocity_new: float32 [2, 128, 256, 128], P(None, 'col', 'slab')
- offsets_new: float32 [2, 128, 256, 128], P(None, 'col', 'slab')
- arrived: float32 [2, 6, 512, 4, 128], P(None, None, 'col', 'slab')
Inputs may be any that keep to these rules, and one draw needn't show every extreme that they name: `counts`: a cell's particles fill its slots 0 to count - 1. `leaving_slot`: a slot of the sending device's own block of cells. `leaving_count`: the block's slots 0 to count - 1 carry particles. `leaving_side`: 0 sends the block to the lower col index, 1 to the higher.
All inputs are finite; a program needn't handle non-finite values.
Results may differ from a plain program's by a relative error of at most 0.0001.
Values sent between devices are 32-bit elements; how exact they have to be, the bound alone decides.
A program may use at most 64 MiB of HBM per device.

v0:
```python
import jax
import jax.numpy as jnp
from jax import lax
from jax.sharding import PartitionSpec as P

ITERS = 3


TIME_STEP = 0.1
REST_DENSITY = 50.0
COMPRESSION = 2.0
RELAXATION = 0.5
GRAVITY = 1.0


def with_halo(array, sides, width):
    for axis, dim in sides:
        peers, length = (lax.axis_size(axis), array.shape[dim])
        up = [(i, (i + 1) % peers) for i in range(peers - 1)]
        down = [(j, i) for i, j in up]
        last = lax.slice_in_dim(array, length - width, length, axis=dim)
        initial = lax.slice_in_dim(array, 0, width, axis=dim)
        before = lax.ppermute(last, axis, up)
        after = lax.ppermute(initial, axis, down)
        array = jnp.concatenate([before, array, after], axis=dim)
    return array


def from_behind(block, axis, distance):
    devices = range(lax.axis_size(axis))
    route = [(i - distance, i) for i in devices if i - distance in devices]
    return lax.ppermute(block, axis, route)


def geometry(center, neighbor, shift_x, shift_z):
    delta_x = center[0][:, :, None] - neighbor[0][:, None, :] - shift_x
    delta_z = center[1][:, :, None] - neighbor[1][:, None, :] - shift_z
    support = jnp.maximum(1.0 - delta_x * delta_x - delta_z * delta_z, 0.0)
    return (delta_x, delta_z, support)


def density_terms(center, neighbor, shift_x, shift_z):
    delta_x, delta_z, support = geometry(center, neighbor, shift_x, shift_z)
    kernel = support * support * support
    slope = 6.0 * support * support
    masses = neighbor[4][:, None, :]
    approach = (center[2][:, :, None] - neighbor[2][:, None, :]) * delta_x + (
        center[3][:, :, None] - neighbor[3][:, None, :]
    ) * delta_z
    return jnp.stack([jnp.sum(masses * kernel, -1), -jnp.sum(masses * slope * approach, -1)])


def jacobi_terms(center, neighbor, shift_x, shift_z):
    delta_x, delta_z, support = geometry(center, neighbor, shift_x, shift_z)
    slope = 6.0 * support * support
    return jnp.stack(
        [jnp.sum(neighbor[2][:, None, :] * slope, -1), jnp.sum(neighbor[3][:, None, :] * slope, -1)]
    )


def update_terms(center, neighbor, shift_x, shift_z):
    delta_x, delta_z, support = geometry(center, neighbor, shift_x, shift_z)
    slope = 6.0 * support * support
    return jnp.sum(neighbor[3][:, None, :] * slope, -1)[None]


def force_terms(center, neighbor, shift_x, shift_z):
    delta_x, delta_z, support = geometry(center, neighbor, shift_x, shift_z)
    slope = 6.0 * support * support
    lifted = neighbor[2][:, None, :] * (neighbor[3][:, None, :] - center[3][:, :, None]) * slope
    return jnp.stack([jnp.sum(lifted * delta_x, -1), jnp.sum(lifted * delta_z, -1)])


def column_pass(extended, column_index, depth_cells, pair_terms):
    column_block = lax.dynamic_slice_in_dim(extended, column_index, 3, 1)
    center = column_block[:, 1, 1 : depth_cells + 1]
    totals = None
    for shift_x in (-1, 0, 1):
        for shift_z in (-1, 0, 1):
            neighbor = column_block[:, 1 + shift_x, 1 + shift_z : 1 + shift_z + depth_cells]
            term = pair_terms(center, neighbor, float(shift_x), float(shift_z))
            totals = term if totals is None else totals + term
    return totals


def sweep(extended, columns, depth_cells, pair_terms):

    def one_column(column_index):
        return column_pass(extended, column_index, depth_cells, pair_terms)

    totals = lax.map(one_column, jnp.arange(columns, dtype=jnp.int32))
    return jnp.moveaxis(totals, 0, 1)


def spread_pressure(pressure):
    deeper = with_halo(pressure, (("slab", 1),), 1)
    return with_halo(deeper, (("col", 0),), 1)


def per_device(
    offsets,
    velocity,
    particle_mass,
    pressure_start,
    counts,
    leaving_slot,
    leaving_count,
    leaving_side,
):
    columns, depth_cells, slot_count = (counts.shape[0], counts.shape[1], offsets.shape[-1])
    alive_mask = jnp.arange(slot_count, dtype=jnp.int32)[None, None, :] < counts[:, :, None]
    live_mass = jnp.where(alive_mask, particle_mass, 0.0)
    base_fields = jnp.concatenate([offsets, velocity, live_mass[None]], 0)
    nearby = with_halo(base_fields, (("col", 1), ("slab", 2)), 1)
    totals = sweep(nearby, columns, depth_cells, density_terms)
    density = jnp.where(alive_mask, totals[0], 0.0)
    diverge = totals[1]
    weight = jnp.where(alive_mask, live_mass / jnp.where(alive_mask, density, 1.0), 0.0)
    weight_ext = with_halo(weight, (("col", 0), ("slab", 1)), 1)
    geometry_ext = nearby[0:2]
    density_ratio = density / REST_DENSITY
    source = jnp.where(
        alive_mask, (density + TIME_STEP * diverge - REST_DENSITY) / REST_DENSITY, 0.0
    )
    pressure = jnp.where(alive_mask, pressure_start, 0.0)
    diagonal = None
    for sweep_index in range(ITERS):
        pressure_ext = spread_pressure(pressure)
        stacked = jnp.concatenate(
            [geometry_ext, weight_ext[None], (weight_ext * pressure_ext)[None]], 0
        )
        if sweep_index == 0:
            totals = sweep(stacked, columns, depth_cells, jacobi_terms)
            diagonal = COMPRESSION + totals[0]
            pulled_sum = totals[1]
        else:
            pulled_sum = sweep(stacked, columns, depth_cells, update_terms)[0]
        updated = (1.0 - RELAXATION) * pressure + RELAXATION * (source + pulled_sum) / diagonal
        pressure = jnp.where(alive_mask, updated, 0.0)
    pressure_ext = spread_pressure(pressure)
    stacked = jnp.concatenate([geometry_ext, weight_ext[None], pressure_ext[None]], 0)
    acceleration = jnp.where(
        alive_mask[None], sweep(stacked, columns, depth_cells, force_terms), 0.0
    )
    pulled = jnp.stack([acceleration[0], acceleration[1] - GRAVITY])
    velocity_new = jnp.where(alive_mask[None], velocity + TIME_STEP * pulled, 0.0)
    offsets_new = jnp.where(alive_mask[None], offsets + TIME_STEP * velocity_new, 0.0)
    state = jnp.concatenate(
        [offsets_new, velocity_new, pressure[None], live_mass[None]], 0
    ).reshape(6, -1)
    block_rows = leaving_slot.shape[0]
    blocks = state[:, leaving_slot.reshape(-1)].reshape(6, block_rows, 1, slot_count)
    filled = jnp.arange(slot_count, dtype=jnp.int32)[None, None, :] < leaving_count[:, :, None]
    upward = jnp.where(filled & (leaving_side[:, :, None] == 1), blocks, 0.0)
    downward = jnp.where(filled & (leaving_side[:, :, None] == 0), blocks, 0.0)
    from_lower = from_behind(upward, "col", 1)
    from_higher = from_behind(downward, "col", -1)
    arrived = jnp.stack([from_lower, from_higher])
    return (density_ratio, pressure, acceleration, velocity_new, offsets_new, arrived)


def solution(mesh):
    return jax.shard_map(
        per_device,
        mesh=mesh,
        in_specs=(
            P(None, "col", "slab", None),
            P(None, "col", "slab", None),
            P("col", "slab", None),
            P("col", "slab", None),
            P("col", "slab"),
            P("col", "slab", None),
            P("col", "slab"),
            P("col", "slab"),
        ),
        out_specs=(
            P("col", "slab", None),
            P("col", "slab", None),
            P(None, "col", "slab", None),
            P(None, "col", "slab", None),
            P(None, "col", "slab", None),
            P(None, None, "col", "slab", None),
        ),
        check_vma=False,
    )
```

profile of v0, /device:TPU:7, one launch (start us, length us, event | category | flops | bytes accessed | tf_op | source)
XLA Modules:
  0.0 521.8 jit_solution(15335759372805819325)
XLA Ops:
  2.6 9.0 %collective-permute-start.1 = (f32[5,1,64,128]{3,2,1,0:T(8,128)S(1)}, f32[5,1,64,128]{3,2,1,0:T(8,128)S(1)}, u32[]{:S(2)}, u32[]{:S(2)}) collective-permute-start(f32[5,1,64,128]{3,2,1,0:T(8,128)S(1)} %get-tuple-element.770), channel_id=1, source_target_pairs={{4,0},{8,4},{12,8},{16,12},{20,16},{24,20},{28,24},{32,28},{36,32}... | collective-permute-start | bytes 491528 | tf_op jit(solution)/shard_map/ppermute | solution.py:24
  14.5 8.6 %collective-permute-done = f32[5,1,64,128]{3,2,1,0:T(8,128)S(1)} collective-permute-done((f32[5,1,64,128]{3,2,1,0:T(8,128)S(1)}, f32[5,1,64,128]{3,2,1,0:T(8,128)S(1)}, u32[]{:S(2)}, u32[]{:S(2)}) %collective-permute-start) | collective-permute-done | bytes 163872 | tf_op jit(solution)/shard_map/ppermute | solution.py:23
  35.5 95.9 %while.70 = (s32[]{:T(128)}, f32[2,2,64,128]{3,2,0,1:T(8,128)S(1)}, s32[2]{0:T(128)S(1)}, f32[5,4,66,128]{3,2,1,0:T(8,128)S(1)}) while((s32[]{:T(128)}, f32[2,2,64,128]{3,2,0,1:T(8,128)S(1)}, s32[2]{0:T(128)S(1)}, f32[5,4,66,128]{3,2,1,0:T(8,128)S(1)}) %tuple.482), condition=%wide.region_19.20_spmd.clone, body=%wide.region_0.19_spmd.sunk.clone | while | flops 210968576 | bytes 6521043 | solution.py:91
  38.4 15.2 %fusion.219 = (f32[64,128]{1,0:T(8,128)S(1)}, f32[64,128]{1,0:T(8,128)S(1)}, f32[64,128]{1,0:T(8,128)S(1)}, f32[64,128]{1,0:T(8,128)S(1)}, f32[64,128]{1,0:T(8,128)S(1)}, /*index=5*/f32[64,128]{1,0:T(8,128)S(1)}) fusion(f32[64,128]{1,0:T(8,128)S(1)} %get-tuple-element.1445, f32[64,128]{1,0:T(8,128)S(1)} %get-tuple-element.1446, ...), kind=kLoop, calls=%fused_computation.63.clone.1.clone | loop fusion | flops 71254016 | bytes 819200 | tf_op jit(solution)/shard_map/while/body/eval_jaxpr/reduce_sum | solution.py:50
  53.6 14.4 %fusion.220 = (f32[64,128]{1,0:T(8,128)S(1)}, f32[64,128]{1,0:T(8,128)S(1)}, f32[64,128]{1,0:T(8,128)S(1)}, f32[64,128]{1,0:T(8,128)S(1)}, f32[64,128]{1,0:T(8,128)S(1)}, /*index=5*/f32[64,128]{1,0:T(8,128)S(1)}) fusion(f32[64,128]{1,0:T(8,128)S(1)} %get-tuple-element.1466, f32[64,128]{1,0:T(8,128)S(1)} %get-tuple-element.1467, ...), kind=kLoop, calls=%fused_computation.71.clone.1.clone | loop fusion | flops 69156864 | bytes 688128 | tf_op jit(solution)/shard_map/while/body/eval_jaxpr/reduce_sum | solution.py:50
  68.0 15.3 %fusion.221 = (f32[64,128]{1,0:T(8,128)S(1)}, f32[64,128]{1,0:T(8,128)S(1)}, f32[64,128]{1,0:T(8,128)S(1)}, f32[64,128]{1,0:T(8,128)S(1)}, f32[64,128]{1,0:T(8,128)S(1)}, /*index=5*/f32[64,128]{1,0:T(8,128)S(1)}) fusion(f32[64,128]{1,0:T(8,128)S(1)} %get-tuple-element.1478, f32[64,128]{1,0:T(8,128)S(1)} %get-tuple-element.1479, ...), kind=kLoop, calls=%fused_computation.68.clone.1.clone | loop fusion | flops 70205440 | bytes 819200 | tf_op jit(solution)/shard_map/while/body/eval_jaxpr/reduce_sum | solution.py:50
  86.3 15.2 %fusion.219 = (f32[64,128]{1,0:T(8,128)S(1)}, f32[64,128]{1,0:T(8,128)S(1)}, f32[64,128]{1,0:T(8,128)S(1)}, f32[64,128]{1,0:T(8,128)S(1)}, f32[64,128]{1,0:T(8,128)S(1)}, /*index=5*/f32[64,128]{1,0:T(8,128)S(1)}) fusion(f32[64,128]{1,0:T(8,128)S(1)} %get-tuple-element.1445, f32[64,128]{1,0:T(8,128)S(1)} %get-tuple-element.1446, ...), kind=kLoop, calls=%fused_computation.63.clone.1.clone | loop fusion | flops 71254016 | bytes 819200 | tf_op jit(solution)/shard_map/while/body/eval_jaxpr/reduce_sum | solution.py:50
  101.5 14.4 %fusion.220 = (f32[64,128]{1,0:T(8,128)S(1)}, f32[64,128]{1,0:T(8,128)S(1)}, f32[64,128]{1,0:T(8,128)S(1)}, f32[64,128]{1,0:T(8,128)S(1)}, f32[64,128]{1,0:T(8,128)S(1)}, /*index=5*/f32[64,128]{1,0:T(8,128)S(1)}) fusion(f32[64,128]{1,0:T(8,128)S(1)} %get-tuple-element.1466, f32[64,128]{1,0:T(8,128)S(1)} %get-tuple-element.1467, ...), kind=kLoop, calls=%fused_computation.71.clone.1.clone | loop fusion | flops 69156864 | bytes 688128 | tf_op jit(solution)/shard_map/while/body/eval_jaxpr/reduce_sum | solution.py:50
  115.9 15.3 %fusion.221 = (f32[64,128]{1,0:T(8,128)S(1)}, f32[64,128]{1,0:T(8,128)S(1)}, f32[64,128]{1,0:T(8,128)S(1)}, f32[64,128]{1,0:T(8,128)S(1)}, f32[64,128]{1,0:T(8,128)S(1)}, /*index=5*/f32[64,128]{1,0:T(8,128)S(1)}) fusion(f32[64,128]{1,0:T(8,128)S(1)} %get-tuple-element.1478, f32[64,128]{1,0:T(8,128)S(1)} %get-tuple-element.1479, ...), kind=kLoop, calls=%fused_computation.68.clone.1.clone | loop fusion | flops 70205440 | bytes 819200 | tf_op jit(solution)/shard_map/while/body/eval_jaxpr/reduce_sum | solution.py:50
  133.4 8.1 %collective-permute-start.8 = (f32[2,1,128]{2,1,0:T(1,128)S(1)}, f32[2,1,128]{2,1,0:T(1,128)S(1)}, u32[]{:S(2)}, u32[]{:S(2)}) collective-permute-start(f32[2,1,128]{2,1,0:T(1,128)S(1)} %get-tuple-element.801), channel_id=1, source_target_pairs={{0,1},{1,2},{2,3},{4,5},{5,6},{6,7},{8,9},{9,10},{10,11},{12,13},{... | collective-permute-start | bytes 3080 | tf_op jit(solution)/shard_map/ppermute | solution.py:23
  166.0 67.0 %while.71 = (s32[]{:T(128)}, f32[2,2,64,128]{3,2,0,1:T(8,128)S(1)}, s32[2]{0:T(128)S(1)}, f32[4,4,66,128]{3,2,1,0:T(8,128)S(1)}) while((s32[]{:T(128)}, f32[2,2,64,128]{3,2,0,1:T(8,128)S(1)}, s32[2]{0:T(128)S(1)}, f32[4,4,66,128]{3,2,1,0:T(8,128)S(1)}) %tuple.485), condition=%wide.region_39.40_spmd.clone, body=%wide.region_20.39_spmd.sunk.clone | while | flops 144834560 | bytes 4849859 | solution.py:91
  168.8 15.6 %multiply_reduce_fusion.40 = (f32[64,128]{1,0:T(8,128)S(1)}, f32[64,128]{1,0:T(8,128)S(1)}, f32[64,128]{1,0:T(8,128)S(1)}, f32[64,128]{1,0:T(8,128)S(1)}, f32[64...) fusion(f32[64,128]{1,0:T(8,128)S(1)} %get-tuple-element.1532, ...), kind=kLoop, calls=%fused_computation.186.clone.1.clone | loop fusion | flops 72278016 | bytes 917504 | tf_op jit(solution)/shard_map/while/body/eval_jaxpr/reduce_sum | solution.py:57
  184.4 15.0 %multiply_reduce_fusion.41 = (f32[64,128]{1,0:T(8,128)S(1)}, f32[64,128]{1,0:T(8,128)S(1)}, f32[64,128]{1,0:T(8,128)S(1)}, f32[64,128]{1,0:T(8,128)S(1)}, f32[64...) fusion(f32[64,128]{1,0:T(8,128)S(1)} %get-tuple-element.1553, ...), kind=kLoop, calls=%fused_computation.184.clone.1.clone | loop fusion | flops 72278016 | bytes 917504 | tf_op jit(solution)/shard_map/while/body/eval_jaxpr/reduce_sum | solution.py:57
  202.3 15.6 %multiply_reduce_fusion.40 = (f32[64,128]{1,0:T(8,128)S(1)}, f32[64,128]{1,0:T(8,128)S(1)}, f32[64,128]{1,0:T(8,128)S(1)}, f32[64,128]{1,0:T(8,128)S(1)}, f32[64...) fusion(f32[64,128]{1,0:T(8,128)S(1)} %get-tuple-element.1532, ...), kind=kLoop, calls=%fused_computation.186.clone.1.clone | loop fusion | flops 72278016 | bytes 917504 | tf_op jit(solution)/shard_map/while/body/eval_jaxpr/reduce_sum | solution.py:57
  217.9 15.0 %multiply_reduce_fusion.41 = (f32[64,128]{1,0:T(8,128)S(1)}, f32[64,128]{1,0:T(8,128)S(1)}, f32[64,128]{1,0:T(8,128)S(1)}, f32[64,128]{1,0:T(8,128)S(1)}, f32[64...) fusion(f32[64,128]{1,0:T(8,128)S(1)} %get-tuple-element.1553, ...), kind=kLoop, calls=%fused_computation.184.clone.1.clone | loop fusion | flops 72278016 | bytes 917504 | tf_op jit(solution)/shard_map/while/body/eval_jaxpr/reduce_sum | solution.py:57
  235.0 8.1 %collective-permute-start.12 = (f32[2,1,128]{2,1,0:T(1,128)S(1)}, f32[2,1,128]{2,1,0:T(1,128)S(1)}, u32[]{:S(2)}, u32[]{:S(2)}) collective-permute-start(f32[2,1,128]{2,1,0:T(1,128)S(1)} %get-tuple-element.797), channel_id=1, source_target_pairs={{0,1},{1,2},{2,3},{4,5},{5,6},{6,7},{8,9},{9,10},{10,11},{12,13},{... | collective-permute-start | bytes 3080 | tf_op jit(solution)/shard_map/ppermute | solution.py:23
  243.9 8.2 %collective-permute-start.15 = (f32[1,66,128]{2,1,0:T(8,128)S(1)}, f32[1,66,128]{2,1,0:T(8,128)S(1)}, u32[]{:S(2)}, u32[]{:S(2)}) collective-permute-start(f32[1,66,128]{2,1,0:T(8,128)S(1)} %get-tuple-element.784), channel_id=1, source_target_pairs={{4,0},{8,4},{12,8},{16,12},{20,16},{24,20},{28,24},{32,28},{36,32}... | collective-permute-start | bytes 101384 | tf_op jit(solution)/shard_map/ppermute | solution.py:24
  261.7 49.0 %while.72 = (s32[]{:T(128)}, f32[2,1,64,128]{3,2,1,0:T(8,128)S(1)}, s32[2]{0:T(128)S(1)}, f32[4,4,66,128]{3,2,1,0:T(8,128)S(1)}) while((s32[]{:T(128)}, f32[2,1,64,128]{3,2,1,0:T(8,128)S(1)}, s32[2]{0:T(128)S(1)}, f32[4,4,66,128]{3,2,1,0:T(8,128)S(1)}) %tuple.488), condition=%wide.region_50.51_spmd.clone, body=%wide.region_40.50_spmd.sunk.clone | while | flops 116383752 | bytes 3342531 | solution.py:91
  264.4 8.0 %fusion.224 = (f32[64,128]{1,0:T(8,128)S(1)}, f32[64,128]{1,0:T(8,128)S(1)}, f32[64,128]{1,0:T(8,128)S(1)}) fusion(f32[64,128]{1,0:T(8,128)S(1)} %get-tuple-element.1601, f32[64,128]{1,0:T(8,128)S(1)} %get-tuple-element.1602, f32[64,128]{1,0:T(8,128)S(1)} %get-tuple-element.1603, f32[64,128]{1,0:T(8,128)S(1)} %get-tuple-element.1604, ...), kind=kLoop, calls=%fused_computation.257.clone.1.clone | loop fusion | flops 39821312 | bytes 458752 | tf_op jit(solution)/shard_map/while/body/eval_jaxpr/reduce_sum | solution.py:64
  272.4 13.8 %fusion.225 = (f32[64,128]{1,0:T(8,128)S(1)}, f32[64,128]{1,0:T(8,128)S(1)}, f32[64,128]{1,0:T(8,128)S(1)}, f32[64,128]{1,0:T(8,128)S(1)}, f32[64,128]{1,0:T(8,128)S(1)}, /*index=5*/f32[64,128]{1,0:T(8,128)S(1)}) fusion(f32[64,128]{1,0:T(8,128)S(1)} %get-tuple-element.1614, f32[64,128]{1,0:T(8,128)S(1)} %get-tuple-element.1615, ...), kind=kLoop, calls=%fused_computation.259.clone.1.clone | loop fusion | flops 76496896 | bytes 786432 | tf_op jit(solution)/shard_map/while/body/eval_jaxpr/reduce_sum | solution.py:64
  296.9 13.8 %fusion.225 = (f32[64,128]{1,0:T(8,128)S(1)}, f32[64,128]{1,0:T(8,128)S(1)}, f32[64,128]{1,0:T(8,128)S(1)}, f32[64,128]{1,0:T(8,128)S(1)}, f32[64,128]{1,0:T(8,128)S(1)}, /*index=5*/f32[64,128]{1,0:T(8,128)S(1)}) fusion(f32[64,128]{1,0:T(8,128)S(1)} %get-tuple-element.1614, f32[64,128]{1,0:T(8,128)S(1)} %get-tuple-element.1615, ...), kind=kLoop, calls=%fused_computation.259.clone.1.clone | loop fusion | flops 76496896 | bytes 786432 | tf_op jit(solution)/shard_map/while/body/eval_jaxpr/reduce_sum | solution.py:64
  312.8 9.5 %collective-permute-start.16 = (f32[2,1,128]{2,1,0:T(1,128)S(1)}, f32[2,1,128]{2,1,0:T(1,128)S(1)}, u32[]{:S(2)}, u32[]{:S(2)}) collective-permute-start(f32[2,1,128]{2,1,0:T(1,128)S(1)} %get-tuple-element.795), channel_id=1, source_target_pairs={{0,1},{1,2},{2,3},{4,5},{5,6},{6,7},{8,9},{9,10},{10,11},{12,13},{... | collective-permute-start | bytes 3080 | tf_op jit(solution)/shard_map/ppermute | solution.py:23
  334.6 49.0 %while.73 = (s32[]{:T(128)}, f32[2,1,64,128]{3,2,1,0:T(8,128)S(1)}, s32[2]{0:T(128)S(1)}, f32[4,4,66,128]{3,2,1,0:T(8,128)S(1)}) while((s32[]{:T(128)}, f32[2,1,64,128]{3,2,1,0:T(8,128)S(1)}, s32[2]{0:T(128)S(1)}, f32[4,4,66,128]{3,2,1,0:T(8,128)S(1)}) %tuple.491), condition=%wide.region_61.62_spmd.clone, body=%wide.region_51.61_spmd.sunk.clone | while | flops 116383752 | bytes 3342531 | solution.py:91
  337.3 8.0 %fusion.226 = (f32[64,128]{1,0:T(8,128)S(1)}, f32[64,128]{1,0:T(8,128)S(1)}, f32[64,128]{1,0:T(8,128)S(1)}) fusion(f32[64,128]{1,0:T(8,128)S(1)} %get-tuple-element.1652, f32[64,128]{1,0:T(8,128)S(1)} %get-tuple-element.1653, f32[64,128]{1,0:T(8,128)S(1)} %get-tuple-element.1654, f32[64,128]{1,0:T(8,128)S(1)} %get-tuple-element.1655, ...), kind=kLoop, calls=%fused_computation.312.clone.1.clone | loop fusion | flops 39821312 | bytes 458752 | tf_op jit(solution)/shard_map/while/body/eval_jaxpr/reduce_sum | solution.py:64
  345.3 13.8 %fusion.227 = (f32[64,128]{1,0:T(8,128)S(1)}, f32[64,128]{1,0:T(8,128)S(1)}, f32[64,128]{1,0:T(8,128)S(1)}, f32[64,128]{1,0:T(8,128)S(1)}, f32[64,128]{1,0:T(8,128)S(1)}, /*index=5*/f32[64,128]{1,0:T(8,128)S(1)}) fusion(f32[64,128]{1,0:T(8,128)S(1)} %get-tuple-element.1665, f32[64,128]{1,0:T(8,128)S(1)} %get-tuple-element.1666, ...), kind=kLoop, calls=%fused_computation.314.clone.1.clone | loop fusion | flops 76496896 | bytes 786432 | tf_op jit(solution)/shard_map/while/body/eval_jaxpr/reduce_sum | solution.py:64
  369.8 13.8 %fusion.227 = (f32[64,128]{1,0:T(8,128)S(1)}, f32[64,128]{1,0:T(8,128)S(1)}, f32[64,128]{1,0:T(8,128)S(1)}, f32[64,128]{1,0:T(8,128)S(1)}, f32[64,128]{1,0:T(8,128)S(1)}, /*index=5*/f32[64,128]{1,0:T(8,128)S(1)}) fusion(f32[64,128]{1,0:T(8,128)S(1)} %get-tuple-element.1665, f32[64,128]{1,0:T(8,128)S(1)} %get-tuple-element.1666, ...), kind=kLoop, calls=%fused_computation.314.clone.1.clone | loop fusion | flops 76496896 | bytes 786432 | tf_op jit(solution)/shard_map/while/body/eval_jaxpr/reduce_sum | solution.py:64
  386.2 9.2 %collective-permute-start.20 = (f32[2,1,128]{2,1,0:T(1,128)S(1)}, f32[2,1,128]{2,1,0:T(1,128)S(1)}, u32[]{:S(2)}, u32[]{:S(2)}) collective-permute-start(f32[2,1,128]{2,1,0:T(1,128)S(1)} %get-tuple-element.793), channel_id=1, source_target_pairs={{0,1},{1,2},{2,3},{4,5},{5,6},{6,7},{8,9},{9,10},{10,11},{12,13},{... | collective-permute-start | bytes 3080 | tf_op jit(solution)/shard_map/ppermute | solution.py:23
  407.8 89.8 %while.74 = (s32[]{:T(128)}, f32[2,2,64,128]{3,2,1,0:T(8,128)S(1)}, s32[2]{0:T(128)S(1)}, f32[4,4,66,128]{3,2,1,0:T(8,128)S(1)}) while((s32[]{:T(128)}, f32[2,2,64,128]{3,2,1,0:T(8,128)S(1)}, s32[2]{0:T(128)S(1)}, f32[4,4,66,128]{3,2,1,0:T(8,128)S(1)}) %tuple.494), condition=%wide.region_81.82_spmd.clone, body=%wide.region_62.81_spmd.sunk.clone | while | flops 163708928 | bytes 4980931 | solution.py:91
  416.8 17.8 %multiply_reduce_fusion.43 = (f32[64,128]{1,0:T(8,128)S(1)}, f32[64,128]{1,0:T(8,128)S(1)}, f32[64,128]{1,0:T(8,128)S(1)}, f32[64,128]{1,0:T(8,128)S(1)}, f32[64...) fusion(f32[64,128]{1,0:T(8,128)S(1)} %get-tuple-element.1712, ...), kind=kLoop, calls=%fused_computation.407.clone.1.clone | loop fusion | flops 73334784 | bytes 884736 | tf_op jit(solution)/shard_map/while/body/eval_jaxpr/reduce_sum | solution.py:71
  434.7 17.9 %multiply_reduce_fusion.44 = (f32[64,128]{1,0:T(8,128)S(1)}, f32[64,128]{1,0:T(8,128)S(1)}, f32[64,128]{1,0:T(8,128)S(1)}, f32[64,128]{1,0:T(8,128)S(1)}, f32[64...) fusion(f32[64,128]{1,0:T(8,128)S(1)} %get-tuple-element.1734, ...), kind=kLoop, calls=%fused_computation.410.clone.1.clone | loop fusion | flops 71237632 | bytes 786432 | tf_op jit(solution)/shard_map/while/body/eval_jaxpr/reduce_sum | solution.py:71
  461.7 17.8 %multiply_reduce_fusion.43 = (f32[64,128]{1,0:T(8,128)S(1)}, f32[64,128]{1,0:T(8,128)S(1)}, f32[64,128]{1,0:T(8,128)S(1)}, f32[64,128]{1,0:T(8,128)S(1)}, f32[64...) fusion(f32[64,128]{1,0:T(8,128)S(1)} %get-tuple-element.1712, ...), kind=kLoop, calls=%fused_computation.407.clone.1.clone | loop fusion | flops 73334784 | bytes 884736 | tf_op jit(solution)/shard_map/while/body/eval_jaxpr/reduce_sum | solution.py:71
  479.5 17.9 %multiply_reduce_fusion.44 = (f32[64,128]{1,0:T(8,128)S(1)}, f32[64,128]{1,0:T(8,128)S(1)}, f32[64,128]{1,0:T(8,128)S(1)}, f32[64,128]{1,0:T(8,128)S(1)}, f32[64...) fusion(f32[64,128]{1,0:T(8,128)S(1)} %get-tuple-element.1734, ...), kind=kLoop, calls=%fused_computation.410.clone.1.clone | loop fusion | flops 71237632 | bytes 786432 | tf_op jit(solution)/shard_map/while/body/eval_jaxpr/reduce_sum | solution.py:71
  (172 shorter events, 146.0 us)
Async XLA Ops:
  2.6 11.9 %collective-permute-start.1 = (f32[5,1,64,128]{3,2,1,0:T(8,128)S(1)}, f32[5,1,64,128]{3,2,1,0:T(8,128)S(1)}, u32[]{:S(2)}, u32[]{:S(2)}) collective-permute-start(f32[5,1,64,128]{3,2,1,0:T(8,128)S(1)} %get-tuple-element.770), channel_id=1, source_target_pairs={{4,0},{8,4},{12,8},{16,12},{20,16},{24,20},{28,24},{32,28},{36,32}... | collective-permute-start | bytes 491528 | tf_op jit(solution)/shard_map/ppermute | solution.py:24
  11.6 11.5 %collective-permute-start = (f32[5,1,64,128]{3,2,1,0:T(8,128)S(1)}, f32[5,1,64,128]{3,2,1,0:T(8,128)S(1)}, u32[]{:S(2)}, u32[]{:S(2)}) collective-permute-start(f32[5,1,64,128]{3,2,1,0:T(8,128)S(1)} %get-tuple-element.769), channel_id=1, source_target_pairs={{0,4},{4,8},{8,12},{12,16},{16,20},{20,24},{24,28},{28,32},{32,36}... | collective-permute-start | bytes 491528 | tf_op jit(solution)/shard_map/ppermute | solution.py:23
  23.9 9.8 %collective-permute-start.3 = (f32[5,4,1,128]{3,2,1,0:T(1,128)S(1)}, f32[5,4,1,128]{3,2,1,0:T(1,128)S(1)}, u32[]{:S(2)}, u32[]{:S(2)}) collective-permute-start(f32[5,4,1,128]{3,2,1,0:T(1,128)S(1)} %get-tuple-element.768), channel_id=1, source_target_pairs={{1,0},{2,1},{3,2},{5,4},{6,5},{7,6},{9,8},{10,9},{11,10},{13,12},{... | collective-permute-start | bytes 30728 | tf_op jit(solution)/shard_map/ppermute | solution.py:24
  27.6 6.8 %collective-permute-start.2 = (f32[5,4,1,128]{3,2,1,0:T(1,128)S(1)}, f32[5,4,1,128]{3,2,1,0:T(1,128)S(1)}, u32[]{:S(2)}, u32[]{:S(2)}) collective-permute-start(f32[5,4,1,128]{3,2,1,0:T(1,128)S(1)} %get-tuple-element.767), channel_id=1, source_target_pairs={{0,1},{1,2},{2,3},{4,5},{5,6},{6,7},{8,9},{9,10},{10,11},{12,13},{... | collective-permute-start | bytes 30728 | tf_op jit(solution)/shard_map/ppermute | solution.py:23
  35.5 95.9 %copy-start.3 = (f32[2,64,128]{2,1,0:T(8,128)S(1)}, f32[2,64,128]{2,1,0:T(8,128)}, u32[]{:S(2)}) copy-start(f32[2,64,128]{2,1,0:T(8,128)} %param.20) | copy-start | bytes 196612
  35.5 95.9 %copy-start.6 = (f32[2,64,128]{2,1,0:T(8,128)S(1)}, f32[2,64,128]{2,1,0:T(8,128)}, u32[]{:S(2)}) copy-start(f32[2,64,128]{2,1,0:T(8,128)} %param.21) | copy-start | bytes 196612
  35.5 95.9 %copy-start.7 = (s32[2,64]{1,0:T(2,128)S(1)}, s32[2,64]{1,0:T(2,128)}, u32[]{:S(2)}) copy-start(s32[2,64]{1,0:T(2,128)} %param.22) | copy-start | bytes 1540
  131.5 15.4 %collective-permute-start.9 = (f32[2,1,128]{2,1,0:T(1,128)S(1)}, f32[2,1,128]{2,1,0:T(1,128)S(1)}, u32[]{:S(2)}, u32[]{:S(2)}) collective-permute-start(f32[2,1,128]{2,1,0:T(1,128)S(1)} %get-tuple-element.802), channel_id=1, source_target_pairs={{1,0},{2,1},{3,2},{5,4},{6,5},{7,6},{9,8},{10,9},{11,10},{13,12},{... | collective-permute-start | bytes 3080 | tf_op jit(solution)/shard_map/ppermute | solution.py:24
  133.4 13.4 %collective-permute-start.8 = (f32[2,1,128]{2,1,0:T(1,128)S(1)}, f32[2,1,128]{2,1,0:T(1,128)S(1)}, u32[]{:S(2)}, u32[]{:S(2)}) collective-permute-start(f32[2,1,128]{2,1,0:T(1,128)S(1)} %get-tuple-element.801), channel_id=1, source_target_pairs={{0,1},{1,2},{2,3},{4,5},{5,6},{6,7},{8,9},{9,10},{10,11},{12,13},{... | collective-permute-start | bytes 3080 | tf_op jit(solution)/shard_map/ppermute | solution.py:23
  141.6 14.0 %collective-permute-start.5 = (f32[1,64,128]{2,1,0:T(8,128)S(1)}, f32[1,64,128]{2,1,0:T(8,128)S(1)}, u32[]{:S(2)}, u32[]{:S(2)}) collective-permute-start(f32[1,64,128]{2,1,0:T(8,128)S(1)} %get-tuple-element.800), channel_id=1, source_target_pairs={{4,0},{8,4},{12,8},{16,12},{20,16},{24,20},{28,24},{32,28},{36,32}... | collective-permute-start | bytes 98312 | tf_op jit(solution)/shard_map/ppermute | solution.py:24
  143.5 12.1 %collective-permute-start.4 = (f32[1,64,128]{2,1,0:T(8,128)S(1)}, f32[1,64,128]{2,1,0:T(8,128)S(1)}, u32[]{:S(2)}, u32[]{:S(2)}) collective-permute-start(f32[1,64,128]{2,1,0:T(8,128)S(1)} %get-tuple-element.799), channel_id=1, source_target_pairs={{0,4},{4,8},{8,12},{12,16},{16,20},{20,24},{24,28},{28,32},{32,36}... | collective-permute-start | bytes 98312 | tf_op jit(solution)/shard_map/ppermute | solution.py:23
  146.9 18.2 %collective-permute-start.11 = (f32[1,66,128]{2,1,0:T(8,128)S(1)}, f32[1,66,128]{2,1,0:T(8,128)S(1)}, u32[]{:S(2)}, u32[]{:S(2)}) collective-permute-start(f32[1,66,128]{2,1,0:T(8,128)S(1)} %get-tuple-element.786), channel_id=1, source_target_pairs={{4,0},{8,4},{12,8},{16,12},{20,16},{24,20},{28,24},{32,28},{36,32}... | collective-permute-start | bytes 101384 | tf_op jit(solution)/shard_map/ppermute | solution.py:24
  153.7 11.5 %collective-permute-start.10 = (f32[1,66,128]{2,1,0:T(8,128)S(1)}, f32[1,66,128]{2,1,0:T(8,128)S(1)}, u32[]{:S(2)}, u32[]{:S(2)}) collective-permute-start(f32[1,66,128]{2,1,0:T(8,128)S(1)} %get-tuple-element.785), channel_id=1, source_target_pairs={{0,4},{4,8},{8,12},{12,16},{16,20},{20,24},{24,28},{28,32},{32,36}... | collective-permute-start | bytes 101384 | tf_op jit(solution)/shard_map/ppermute | solution.py:23
  155.7 9.5 %collective-permute-start.7 = (f32[4,1,128]{2,1,0:T(1,128)S(1)}, f32[4,1,128]{2,1,0:T(1,128)S(1)}, u32[]{:S(2)}, u32[]{:S(2)}) collective-permute-start(f32[4,1,128]{2,1,0:T(1,128)S(1)} %get-tuple-element.776), channel_id=1, source_target_pairs={{1,0},{2,1},{3,2},{5,4},{6,5},{7,6},{9,8},{10,9},{11,10},{13,12},{... | collective-permute-start | bytes 6152 | tf_op jit(solution)/shard_map/ppermute | solution.py:24
  157.6 8.3 %collective-permute-start.6 = (f32[4,1,128]{2,1,0:T(1,128)S(1)}, f32[4,1,128]{2,1,0:T(1,128)S(1)}, u32[]{:S(2)}, u32[]{:S(2)}) collective-permute-start(f32[4,1,128]{2,1,0:T(1,128)S(1)} %get-tuple-element.775), channel_id=1, source_target_pairs={{0,1},{1,2},{2,3},{4,5},{5,6},{6,7},{8,9},{9,10},{10,11},{12,13},{... | collective-permute-start | bytes 6152 | tf_op jit(solution)/shard_map/ppermute | solution.py:23
  233.1 10.1 %collective-permute-start.13 = (f32[2,1,128]{2,1,0:T(1,128)S(1)}, f32[2,1,128]{2,1,0:T(1,128)S(1)}, u32[]{:S(2)}, u32[]{:S(2)}) collective-permute-start(f32[2,1,128]{2,1,0:T(1,128)S(1)} %get-tuple-element.798), channel_id=1, source_target_pairs={{1,0},{2,1},{3,2},{5,4},{6,5},{7,6},{9,8},{10,9},{11,10},{13,12},{... | collective-permute-start | bytes 3080 | tf_op jit(solution)/shard_map/ppermute | solution.py:24
  235.0 8.8 %collective-permute-start.12 = (f32[2,1,128]{2,1,0:T(1,128)S(1)}, f32[2,1,128]{2,1,0:T(1,128)S(1)}, u32[]{:S(2)}, u32[]{:S(2)}) collective-permute-start(f32[2,1,128]{2,1,0:T(1,128)S(1)} %get-tuple-element.797), channel_id=1, source_target_pairs={{0,1},{1,2},{2,3},{4,5},{5,6},{6,7},{8,9},{9,10},{10,11},{12,13},{... | collective-permute-start | bytes 3080 | tf_op jit(solution)/shard_map/ppermute | solution.py:23
  243.9 10.4 %collective-permute-start.15 = (f32[1,66,128]{2,1,0:T(8,128)S(1)}, f32[1,66,128]{2,1,0:T(8,128)S(1)}, u32[]{:S(2)}, u32[]{:S(2)}) collective-permute-start(f32[1,66,128]{2,1,0:T(8,128)S(1)} %get-tuple-element.784), channel_id=1, source_target_pairs={{4,0},{8,4},{12,8},{16,12},{20,16},{24,20},{28,24},{32,28},{36,32}... | collective-permute-start | bytes 101384 | tf_op jit(solution)/shard_map/ppermute | solution.py:24
  252.1 9.5 %collective-permute-start.14 = (f32[1,66,128]{2,1,0:T(8,128)S(1)}, f32[1,66,128]{2,1,0:T(8,128)S(1)}, u32[]{:S(2)}, u32[]{:S(2)}) collective-permute-start(f32[1,66,128]{2,1,0:T(8,128)S(1)} %get-tuple-element.783), channel_id=1, source_target_pairs={{0,4},{4,8},{8,12},{12,16},{16,20},{20,24},{24,28},{28,32},{32,36}... | collective-permute-start | bytes 101384 | tf_op jit(solution)/shard_map/ppermute | solution.py:23
  310.8 11.5 %collective-permute-start.17 = (f32[2,1,128]{2,1,0:T(1,128)S(1)}, f32[2,1,128]{2,1,0:T(1,128)S(1)}, u32[]{:S(2)}, u32[]{:S(2)}) collective-permute-start(f32[2,1,128]{2,1,0:T(1,128)S(1)} %get-tuple-element.796), channel_id=1, source_target_pairs={{1,0},{2,1},{3,2},{5,4},{6,5},{7,6},{9,8},{10,9},{11,10},{13,12},{... | collective-permute-start | bytes 3080 | tf_op jit(solution)/shard_map/ppermute | solution.py:24
  312.8 10.2 %collective-permute-start.16 = (f32[2,1,128]{2,1,0:T(1,128)S(1)}, f32[2,1,128]{2,1,0:T(1,128)S(1)}, u32[]{:S(2)}, u32[]{:S(2)}) collective-permute-start(f32[2,1,128]{2,1,0:T(1,128)S(1)} %get-tuple-element.795), channel_id=1, source_target_pairs={{0,1},{1,2},{2,3},{4,5},{5,6},{6,7},{8,9},{9,10},{10,11},{12,13},{... | collective-permute-start | bytes 3080 | tf_op jit(solution)/shard_map/ppermute | solution.py:23
  323.0 5.3 %collective-permute-start.19 = (f32[1,66,128]{2,1,0:T(8,128)S(1)}, f32[1,66,128]{2,1,0:T(8,128)S(1)}, u32[]{:S(2)}, u32[]{:S(2)}) collective-permute-start(f32[1,66,128]{2,1,0:T(8,128)S(1)} %get-tuple-element.782), channel_id=1, source_target_pairs={{4,0},{8,4},{12,8},{16,12},{20,16},{24,20},{28,24},{32,28},{36,32}... | collective-permute-start | bytes 101384 | tf_op jit(solution)/shard_map/ppermute | solution.py:24
  324.9 9.5 %collective-permute-start.18 = (f32[1,66,128]{2,1,0:T(8,128)S(1)}, f32[1,66,128]{2,1,0:T(8,128)S(1)}, u32[]{:S(2)}, u32[]{:S(2)}) collective-permute-start(f32[1,66,128]{2,1,0:T(8,128)S(1)} %get-tuple-element.781), channel_id=1, source_target_pairs={{0,4},{4,8},{8,12},{12,16},{16,20},{20,24},{24,28},{28,32},{32,36}... | collective-permute-start | bytes 101384 | tf_op jit(solution)/shard_map/ppermute | solution.py:23
  384.3 113.6 %copy-start.2 = (f32[2,64,128]{2,1,0:T(8,128)}, f32[2,64,128]{2,1,0:T(8,128)S(1)}, u32[]{:S(2)}) copy-start(f32[2,64,128]{2,1,0:T(8,128)S(1)} %get-tuple-element.771) | copy-start | bytes 196612
  384.3 11.2 %collective-permute-start.21 = (f32[2,1,128]{2,1,0:T(1,128)S(1)}, f32[2,1,128]{2,1,0:T(1,128)S(1)}, u32[]{:S(2)}, u32[]{:S(2)}) collective-permute-start(f32[2,1,128]{2,1,0:T(1,128)S(1)} %get-tuple-element.794), channel_id=1, source_target_pairs={{1,0},{2,1},{3,2},{5,4},{6,5},{7,6},{9,8},{10,9},{11,10},{13,12},{... | collective-permute-start | bytes 3080 | tf_op jit(solution)/shard_map/ppermute | solution.py:24
  386.2 10.0 %collective-permute-start.20 = (f32[2,1,128]{2,1,0:T(1,128)S(1)}, f32[2,1,128]{2,1,0:T(1,128)S(1)}, u32[]{:S(2)}, u32[]{:S(2)}) collective-permute-start(f32[2,1,128]{2,1,0:T(1,128)S(1)} %get-tuple-element.793), channel_id=1, source_target_pairs={{0,1},{1,2},{2,3},{4,5},{5,6},{6,7},{8,9},{9,10},{10,11},{12,13},{... | collective-permute-start | bytes 3080 | tf_op jit(solution)/shard_map/ppermute | solution.py:23
  396.2 5.4 %collective-permute-start.23 = (f32[1,66,128]{2,1,0:T(8,128)S(1)}, f32[1,66,128]{2,1,0:T(8,128)S(1)}, u32[]{:S(2)}, u32[]{:S(2)}) collective-permute-start(f32[1,66,128]{2,1,0:T(8,128)S(1)} %get-tuple-element.780), channel_id=1, source_target_pairs={{4,0},{8,4},{12,8},{16,12},{20,16},{24,20},{28,24},{32,28},{36,32}... | collective-permute-start | bytes 101384 | tf_op jit(solution)/shard_map/ppermute | solution.py:24
  398.2 9.5 %collective-permute-start.22 = (f32[1,66,128]{2,1,0:T(8,128)S(1)}, f32[1,66,128]{2,1,0:T(8,128)S(1)}, u32[]{:S(2)}, u32[]{:S(2)}) collective-permute-start(f32[1,66,128]{2,1,0:T(8,128)S(1)} %get-tuple-element.779), channel_id=1, source_target_pairs={{0,4},{4,8},{8,12},{12,16},{16,20},{20,24},{24,28},{28,32},{32,36}... | collective-permute-start | bytes 101384 | tf_op jit(solution)/shard_map/ppermute | solution.py:23
  407.8 89.8 %copy-start = (f32[2,2,64,128]{3,2,1,0:T(8,128)S(1)}, f32[2,2,64,128]{3,2,1,0:T(8,128)}, u32[]{:S(2)}) copy-start(f32[2,2,64,128]{3,2,1,0:T(8,128)} %param.19) | copy-start | bytes 393220
  407.8 89.8 %copy-start.1 = (f32[2,2,64,128]{3,2,1,0:T(8,128)S(1)}, f32[2,2,64,128]{3,2,1,0:T(8,128)}, u32[]{:S(2)}) copy-start(f32[2,2,64,128]{3,2,1,0:T(8,128)} %param.18) | copy-start | bytes 393220
  509.8 6.0 %collective-permute-start.25 = (f32[6,8,1,128]{3,1,0,2:T(8,128)S(1)}, f32[6,8,1,128]{3,1,0,2:T(8,128)S(1)}, u32[]{:S(2)}, u32[]{:S(2)}) collective-permute-start(f32[6,8,1,128]{3,1,0,2:T(8,128)S(1)} %get-tuple-element.804), channel_id=1, source_target_pairs={{4,0},{8,4},{12,8},{16,12},{20,16},{24,20},{28,24},{32,28},{36,32}... | collective-permute-start | bytes 73736 | tf_op jit(solution)/shard_map/ppermute | solution.py:32
  511.8 9.4 %collective-permute-start.24 = (f32[6,8,1,128]{3,1,0,2:T(8,128)S(1)}, f32[6,8,1,128]{3,1,0,2:T(8,128)S(1)}, u32[]{:S(2)}, u32[]{:S(2)}) collective-permute-start(f32[6,8,1,128]{3,1,0,2:T(8,128)S(1)} %get-tuple-element.803), channel_id=1, source_target_pairs={{0,4},{4,8},{8,12},{12,16},{16,20},{20,24},{24,28},{28,32},{32,36}... | collective-permute-start | bytes 73736 | tf_op jit(solution)/shard_map/ppermute | solution.py:32
  (5 other events, 200.1 us)
where the time goes:
time: 524 us; the launch traced here: 522 us
  other arithmetic  329 us (63%)
  starting transfers between devices  113 us (22%)
  waiting for transfers between devices  37.8 us (7%)
  local copies, waits for them, and re-layouts  20.8 us (4%)
  loops' own time  20 us (4%)
    reduce_sum x6, other arithmetic, density_terms(): jnp.sum(masses * kernel, -1)  89.8 us
    reduce_sum x8, other arithmetic, update_terms(): return jnp.sum(neighbor[3][:, None, :] * slope, -1)[None]  87 us
    reduce_sum x6, other arithmetic, force_terms(): jnp.sum(lifted * delta_x, -1)  84.1 us
    ppermute x12, starting transfers between devices, with_halo(): before = lax.ppermute(last, axis, up)  64.6 us
    reduce_sum x4, other arithmetic, jacobi_terms(): jnp.sum(neighbor[2][:, None, :] * slope, -1)  61.3 us
    ppermute x12, starting transfers between devices, with_halo(): after = lax.ppermute(initial, axis, down)  42.9 us
    ppermute x12, waiting for transfers between devices, with_halo(): before = lax.ppermute(last, axis, up)  31.4 us
    another operation x5, loops' own time, sweep(): totals = lax.map(one_column, jnp.arange(columns, dtype=jnp.int32))  20 us
  transfers between devices with their start and end apart: 26, of which 11 were waited for; matrix products, arithmetic and copies ran while one was open for 0% of the time, Pallas kernels for 0%

commit v1 on v0

v1 whole, which is shorter than its diff:
```python
import functools

import jax
import jax.numpy as jnp
from jax import lax
from jax.experimental import pallas as pl
from jax.experimental.pallas import tpu as pltpu
from jax.sharding import PartitionSpec as P

ITERS = 3
TIME_STEP = 0.1
REST_DENSITY = 50.0
COMPRESSION = 2.0
RELAXATION = 0.5
GRAVITY = 1.0

MESH = pl.DeviceIdType.MESH
F32 = jnp.float32

X, Z, VX, VZ, MASS, P0, WEIGHT, P1, P2, P3 = range(10)
FIRST = 8
CELLS = 64
SLOTS = 128
BLOCKS = 16

OWN_TILES = (
    ((1, 0, False, True), (1, 1, True, True), (2, -1, True, True), (2, 0, True, True), (2, 1, True, True)),
    ((2, 0, False, True), (2, 1, True, True)),
)
HALO_TILES = (
    ((1, 1, True, False), (1, 0, True, False), (1, -1, True, False)),
    ((2, 1, True, False), (2, 0, True, False), (2, -1, True, False)),
)
EXTRA = (
    (1, -1, ((1, 1, True, False), (2, 1, True, False))),
    (2, -1, ((2, 1, True, False),)),
    (1, CELLS, ((2, -1, True, False),)),
)
OWN0, OWN1, EXTRA0, HALO0, HALO1 = 0, 320, 448, 452, 650
TILES = 848
PAD = 2
FIELDS = 5


class Phase:
    def __init__(self, outs, a_fields, b_rows, shared, b_factors, a_factors):
        self.outs = outs
        self.a_fields = a_fields
        self.b_rows = b_rows
        self.shared = shared
        self.b_factors = b_factors
        self.a_factors = a_factors


def kernel(
    base,
    edges,
    leaving_slot,
    leaving_count,
    leaving_side,
    ratio_out,
    pressure_out,
    accel_out,
    velocity_out,
    offsets_out,
    arrived_out,
    rows,
    slopes,
    columns,
    kept,
    lane_columns,
    lane_sums,
    column_sums,
    row_sums,
    edge_send,
    edge_recv_base,
    edge_recv,
    block_send,
    block_recv,
    local_sem,
    send_sem,
    recv_sem,
    *,
    n_col,
    n_slab,
):
    col = lax.axis_index("col")
    slab = lax.axis_index("slab")
    around = ((-1, 0), (1, 0), (0, -1), (0, 1), (-1, -1), (-1, 1), (1, -1), (1, 1))

    def there(shift):
        ok = None
        for size, me, step in ((n_col, col, shift[0]), (n_slab, slab, shift[1])):
            if step:
                one = (me > 0) if step < 0 else (me < size - 1)
                ok = one if ok is None else jnp.logical_and(ok, one)
        return ok

    def device(shift):
        return (col + shift[0], slab + shift[1])

    local = pltpu.make_async_copy(base, rows.at[X : P0 + 1, 1:3, FIRST : FIRST + CELLS, :], local_sem.at[0])
    local.start()

    zeros = jnp.zeros((8, SLOTS), F32)
    for field in range(10):
        for column in range(4):
            if column in (0, 3):

                def clear(i, carry, field=field, column=column):
                    rows[field, column, pl.ds(pl.multiple_of(i * 8, 8), 8), :] = zeros
                    return carry

                lax.fori_loop(0, 10, clear, 0)
            else:
                rows[field, column, 0:8, :] = zeros
                rows[field, column, FIRST + CELLS : FIRST + CELLS + 8, :] = zeros
    edge_recv_base[...] = jnp.zeros_like(edge_recv_base)
    edge_recv[...] = jnp.zeros_like(edge_recv)
    block_recv[...] = jnp.zeros_like(block_recv)
    for place in range(4):
        for o in (0, 1):
            lane_sums[place, o] = jnp.zeros((BLOCKS, 8, SLOTS), F32)
    for o in (0, 1):
        for c in (0, 1):
            column_sums[o, c] = jnp.zeros((SLOTS, SLOTS), F32)
    for place in range(7):
        for column in range(4):
            columns[place, column] = jnp.zeros((SLOTS, SLOTS), F32)

    barrier = pltpu.get_barrier_semaphore()
    for shift in around:

        @pl.when(there(shift))
        def _(shift=shift):
            pl.semaphore_signal(barrier, inc=1, device_id=device(shift), device_id_type=MESH)

    peers = sum(jnp.where(there(shift), 1, 0).astype(jnp.int32) for shift in around)
    pl.semaphore_wait(barrier, peers)

    def copy_of(step, n):
        shift = around[n]
        back = around.index((-shift[0], -shift[1]))
        if n < 2:
            own, far = (1, 3) if n == 0 else (2, 0)
            if step == 0:
                src = base.at[:, own - 1]
                dst = rows.at[X : P0 + 1, far, FIRST : FIRST + CELLS, :]
            else:
                src = rows.at[P0 + step, own, FIRST : FIRST + CELLS, :]
                dst = rows.at[P0 + step, far, FIRST : FIRST + CELLS, :]
        else:
            side = 0 if shift[1] < 0 else 1
            if step == 0:
                src = edges.at[side]
                dst = edge_recv_base.at[back - 2]
            else:
                src = edge_send.at[step - 1, side]
                dst = edge_recv.at[step - 1, back - 2]
        return shift, pltpu.make_async_remote_copy(
            src_ref=src,
            dst_ref=dst,
            send_sem=send_sem.at[step, n],
            recv_sem=recv_sem.at[step, back],
            device_id=device(shift),
            device_id_type=MESH,
        )

    def send(step):
        if step > 0:
            for side, at in ((0, FIRST), (1, FIRST + CELLS - 1)):
                for c in (0, 1):
                    edge_send[step - 1, side, c : c + 1, :] = rows[P0 + step, 1 + c, at : at + 1, :]
        for n in (2, 3, 0, 1, 4, 5, 6, 7):
            shift, copy = copy_of(step, n)

            @pl.when(there(shift))
            def _(copy=copy):
                copy.start()

    def receive(step, which):
        for n in which:
            shift, _ = copy_of(step, n)
            back = around.index((-shift[0], -shift[1]))
            _, mirror = copy_of(step, back)

            @pl.when(there(shift))
            def _(mirror=mirror):
                mirror.wait_recv()

        for n in which:
            if n < 2:
                continue
            shift = around[n]
            at = FIRST - 1 if shift[1] < 0 else FIRST + CELLS
            take = {0: ((1, 0), (2, 1)), -1: ((0, 1),), 1: ((3, 0),)}[shift[0]]
            for mine, theirs in take:
                if step == 0:
                    for field in range(6):
                        at_row = field * 2 + theirs
                        rows[field, mine, at : at + 1, :] = edge_recv_base[n - 2, at_row : at_row + 1, :]
                else:
                    rows[P0 + step, mine, at : at + 1, :] = edge_recv[step - 1, n - 2, theirs : theirs + 1, :]

    def finish_sends(step):
        for n in range(8):
            shift, copy = copy_of(step, n)

            @pl.when(there(shift))
            def _(copy=copy):
                copy.wait_send()

    def own_rows(field):
        return jnp.concatenate([rows[field, c, FIRST : FIRST + CELLS, :] for c in (1, 2)], axis=0)

    def set_own(field, value):
        for c in (0, 1):
            rows[field, 1 + c, FIRST : FIRST + CELLS, :] = value[c * CELLS : (c + 1) * CELLS]

    def prepare(phase, column, k, place):
        lane = jnp.full((8, SLOTS), k + FIRST, jnp.int32)
        for b in range(BLOCKS):
            for i, field in enumerate(phase.a_fields):
                part = columns[field, column, b * 8 : b * 8 + 8, :]
                lane_columns[place, i, b] = jnp.take_along_axis(part, lane, axis=1)

    def compute(phase, column, k, tiles, tile0, place):
        outs = phase.outs
        b_rows, theirs = [], []
        for other, dk, _, _ in tiles:

            def row(field, other=other, dk=dk):
                return jnp.broadcast_to(rows[field, other, pl.ds(k + (FIRST + dk), 1), :], (8, SLOTS))

            b_rows.append(phase.b_rows(row, float(other - column), float(dk)))
            theirs.append([[None, None] for _ in range(outs)])
        for b in range(BLOCKS):
            a = [lane_columns[place, i, b] for i in range(len(phase.a_fields))]
            a_factors = phase.a_factors(a)
            mine = [None] * outs
            for i, (_, _, give, take) in enumerate(tiles):
                shared = phase.shared(a, b_rows[i], (tile0 + i, slice(b * 8, b * 8 + 8)))
                for o in range(outs):
                    if take:
                        term = shared[o] * phase.b_factors(b_rows[i])[o]
                        mine[o] = term if mine[o] is None else mine[o] + term
                    if give:
                        term = shared[o] * a_factors[o]
                        so_far = theirs[i][o][b % 2]
                        theirs[i][o][b % 2] = term if so_far is None else so_far + term
            for o in range(outs):
                if mine[o] is not None:
                    lane_sums[place, o, b] = mine[o]
        for i, (other, dk, give, _) in enumerate(tiles):
            if give:
                for o in range(outs):
                    at = (o, other - 1, k + (PAD + dk))
                    row_sums[at] = row_sums[at] + (theirs[i][o][0] + theirs[i][o][1])

    def collect(phase, column, k, place):
        here = lax.broadcasted_iota(jnp.int32, (8, SLOTS), 1) == k + FIRST
        for b in range(BLOCKS):
            for o in range(phase.outs):
                total = jnp.sum(lane_sums[place, o, b], axis=1, keepdims=True)
                at = (o, column - 1, slice(b * 8, b * 8 + 8), slice(None))
                column_sums[at] = jnp.where(here, total, column_sums[at])

    def run(phase, step, transpose):
        def clear(i, carry):
            for o in range(phase.outs):
                row_sums[o, 0, i] = zeros
                row_sums[o, 1, i] = zeros
            return carry

        lax.fori_loop(0, CELLS + 2 * PAD, clear, 0)
        transpose((1, 2))

        def prepare_own(k, parity):
            prepare(phase, 1, k, 2 * parity)
            prepare(phase, 2, k, 2 * parity + 1)

        def compute_own(k, parity):
            compute(phase, 1, k, OWN_TILES[0], OWN0 + 5 * k, 2 * parity)
            compute(phase, 2, k, OWN_TILES[1], OWN1 + 2 * k, 2 * parity + 1)

        def collect_own(k, parity):
            collect(phase, 1, k, 2 * parity)
            collect(phase, 2, k, 2 * parity + 1)

        def own(i, carry):
            for parity in (0, 1):
                k = 1 + 2 * i + parity
                prepare_own(k + 1, 1 - parity)
                collect_own(k - 1, 1 - parity)
                compute_own(k, parity)
            return carry

        prepare_own(1, 0)
        lax.fori_loop(0, (CELLS - 2) // 2, own, 0)
        collect_own(CELLS - 2, 1)

        receive(step, range(8))
        transpose((0, 1, 2, 3))

        def ends(i, carry):
            k = i * (CELLS - 1)
            prepare_own(k, 0)
            compute_own(k, 0)
            collect_own(k, 0)
            return carry

        lax.fori_loop(0, 2, ends, 0)
        for i, (column, k, _) in enumerate(EXTRA):
            prepare(phase, column, k, i)
        tile0 = EXTRA0
        for i, (column, k, tiles) in enumerate(EXTRA):
            compute(phase, column, k, tiles, tile0, i)
            tile0 += len(tiles)

        def prepare_halo(k, parity):
            prepare(phase, 0, k, 2 * parity)
            prepare(phase, 3, k, 2 * parity + 1)

        def halo(i, carry):
            for parity in (0, 1):
                k = 2 * i + parity - 1
                prepare_halo(k + 1, 1 - parity)
                compute(phase, 0, k, HALO_TILES[0], HALO0 + 3 * (k + 1), 2 * parity)
                compute(phase, 3, k, HALO_TILES[1], HALO1 + 3 * (k + 1), 2 * parity + 1)
            return carry

        prepare_halo(-1, 0)
        lax.fori_loop(0, (CELLS + 2) // 2, halo, 0)

    def sums(o):
        parts = []
        for c in (0, 1):
            by_row = jnp.sum(row_sums[o, c, PAD : PAD + CELLS], axis=1)
            parts.append(by_row + column_sums[o, c].T[FIRST : FIRST + CELLS])
        return jnp.concatenate(parts, axis=0)

    def transpose_of(pairs):
        def of(which):
            for column in which:
                for place, value in pairs:
                    columns[place, column, :, 0:80] = value(column).T

        return of

    def field(f):
        return lambda column: rows[f, column]

    def product(f):
        return lambda column: rows[WEIGHT, column] * rows[f, column]

    def geometry_rows(row, shift_x, shift_z):
        return row(X) + shift_x, row(Z) + shift_z

    def density_rows(row, shift_x, shift_z):
        return (*geometry_rows(row, shift_x, shift_z), row(VX), row(VZ), row(MASS))

    def density_shared(a, b, at):
        dx = a[0] - b[0]
        dz = a[1] - b[1]
        support = jnp.maximum(1.0 - (dx * dx + dz * dz), 0.0)
        square = support * support
        slopes[at] = square
        approach = (a[2] - b[2]) * dx + (a[3] - b[3]) * dz
        return square * support, square * approach

    def first_rows(row, shift_x, shift_z):
        weight = row(WEIGHT)
        return weight, weight * row(P0)

    def next_rows(pressure_field):
        def of(row, shift_x, shift_z):
            return (row(WEIGHT) * row(pressure_field),)

        return of

    def force_rows(row, shift_x, shift_z):
        return (*geometry_rows(row, shift_x, shift_z), row(WEIGHT), row(P3))

    def force_shared(a, b, at):
        lifted = slopes[at] * (b[3] - a[3])
        return lifted * (a[0] - b[0]), lifted * (a[1] - b[1])

    def repeat(part, times):
        return lambda values: (values[part],) * times

    CW, CQ, CP = 4, 5, 6

    send(0)
    local.wait()
    run(
        Phase(2, (0, 1, 2, 3, 4), density_rows, density_shared, repeat(4, 2), repeat(4, 2)),
        0,
        transpose_of([(f, field(f)) for f in (X, Z, VX, VZ, MASS)]),
    )
    live_mass = own_rows(MASS)
    alive = live_mass > 0.0
    density = jnp.where(alive, sums(0), 0.0)
    diverge = -6.0 * sums(1)
    ratio = density / REST_DENSITY
    for c in (0, 1):
        ratio_out[c] = ratio[c * CELLS : (c + 1) * CELLS]
    weight = jnp.where(alive, 6.0 * live_mass / jnp.where(alive, density, 1.0), 0.0)
    set_own(WEIGHT, weight)
    send(1)
    kept[0] = jnp.where(alive, (density + TIME_STEP * diverge - REST_DENSITY) / REST_DENSITY, 0.0)
    for sweep in range(ITERS):
        pressure_field = P0 if sweep == 0 else P0 + 1 + sweep
        if sweep == 0:
            phase = Phase(
                2,
                (CW, CQ),
                first_rows,
                lambda a, b, at: (slopes[at],) * 2,
                lambda b: b,
                lambda a: a,
            )
            moved = [(CW, field(WEIGHT)), (CQ, product(P0))]
        else:
            phase = Phase(
                1,
                (CQ,),
                next_rows(pressure_field),
                lambda a, b, at: (slopes[at],),
                lambda b: b,
                lambda a: a,
            )
            moved = [(CQ, product(pressure_field))]
        run(phase, 1 + sweep, transpose_of(moved))
        if sweep == 0:
            kept[1] = COMPRESSION + sums(0)
            pulled = sums(1)
        else:
            pulled = sums(0)
        updated = (1.0 - RELAXATION) * own_rows(pressure_field) + RELAXATION * (kept[0] + pulled) / kept[1]
        pressure = jnp.where(own_rows(MASS) > 0.0, updated, 0.0)
        set_own(P1 + sweep, pressure)
        send(2 + sweep)
    for c in (0, 1):
        pressure_out[c] = pressure[c * CELLS : (c + 1) * CELLS]
    run(
        Phase(2, (X, Z, CW, CP), force_rows, force_shared, repeat(2, 2), repeat(2, 2)),
        4,
        transpose_of([(CP, field(P3))]),
    )

    live_mass = own_rows(MASS)
    alive = live_mass > 0.0
    for o in (0, 1):
        accel = jnp.where(alive, sums(o), 0.0)
        pulled = accel - GRAVITY if o == 1 else accel
        velocity_new = jnp.where(alive, own_rows(VX + o) + TIME_STEP * pulled, 0.0)
        offsets_new = jnp.where(alive, own_rows(X + o) + TIME_STEP * velocity_new, 0.0)
        for c in (0, 1):
            part = slice(c * CELLS, (c + 1) * CELLS)
            accel_out[o, c] = accel[part]
            velocity_out[o, c] = velocity_new[part]
            offsets_out[o, c] = offsets_new[part]
        columns[o, 0] = offsets_new.T
        columns[2 + o, 0] = velocity_new.T
    columns[4, 0] = own_rows(P3).T
    columns[5, 0] = live_mass.T

    chosen = leaving_slot[...]
    cell = chosen // SLOTS
    slot = chosen - cell * SLOTS
    lanes = lax.broadcasted_iota(jnp.int32, (8, SLOTS), 1)
    filled = lanes < leaving_count[...]
    upward = filled & (leaving_side[...] == 1)
    downward = filled & (leaving_side[...] == 0)
    sublanes = lax.broadcasted_iota(jnp.int32, (SLOTS, SLOTS), 0)
    cell_is, slot_is = [], []
    for b in range(8):
        cell_is.append(jnp.where(sublanes == cell[b : b + 1], 1.0, 0.0).astype(jnp.bfloat16))
    for comp in range(6):
        value = columns[comp, 0]
        high = value.astype(jnp.bfloat16)
        rest = value - high.astype(F32)
        middle = rest.astype(jnp.bfloat16)
        low = (rest - middle.astype(F32)).astype(jnp.bfloat16)
        picked = []
        for b in range(8):
            by_slot = sum(
                jnp.dot(part, cell_is[b], preferred_element_type=F32) for part in (low, middle, high)
            )
            one = jnp.where(sublanes == slot[b : b + 1], by_slot, 0.0)
            picked.append(jnp.sum(one, axis=0, keepdims=True))
        block = jnp.concatenate(picked, axis=0)
        block_send[0, comp] = jnp.where(downward, block, 0.0)
        block_send[1, comp] = jnp.where(upward, block, 0.0)

    def block_copy(n):
        return around[n], pltpu.make_async_remote_copy(
            src_ref=block_send.at[n],
            dst_ref=block_recv.at[1 - n],
            send_sem=send_sem.at[5, n],
            recv_sem=recv_sem.at[5, 1 - n],
            device_id=device(around[n]),
            device_id_type=MESH,
        )

    for n in (0, 1):
        shift, copy = block_copy(n)

        @pl.when(there(shift))
        def _(copy=copy):
            copy.start()

    for step in range(5):
        finish_sends(step)
    for n in (0, 1):
        shift, copy = block_copy(n)
        _, mirror = block_copy(1 - n)

        @pl.when(there(shift))
        def _(copy=copy, mirror=mirror):
            mirror.wait_recv()
            copy.wait_send()

    arrived_out[...] = block_recv[...]


def per_device(
    n_col,
    n_slab,
    offsets,
    velocity,
    particle_mass,
    pressure_start,
    counts,
    leaving_slot,
    leaving_count,
    leaving_side,
):
    alive = jnp.arange(SLOTS, dtype=jnp.int32)[None, None, :] < counts[:, :, None]
    live_mass = jnp.where(alive, particle_mass, 0.0)
    pressure = jnp.where(alive, pressure_start, 0.0)
    base = jnp.concatenate([offsets, velocity, live_mass[None], pressure[None]], 0)
    edges = jnp.stack([base[:, :, 0].reshape(12, SLOTS), base[:, :, CELLS - 1].reshape(12, SLOTS)])
    edges = jnp.pad(edges, ((0, 0), (0, 4), (0, 0)))
    vmem = pl.BlockSpec(memory_space=pltpu.VMEM)
    anywhere = pl.BlockSpec(memory_space=pl.ANY)
    cells = (2, CELLS, SLOTS)
    shape = lambda *s: jax.ShapeDtypeStruct(s, F32)
    results = pl.pallas_call(
        functools.partial(kernel, n_col=n_col, n_slab=n_slab),
        out_shape=(shape(*cells), shape(*cells), shape(2, *cells), shape(2, *cells), shape(2, *cells), shape(2, 6, 8, SLOTS)),
        in_specs=[anywhere, anywhere, vmem, vmem, vmem],
        out_specs=[vmem] * 6,
        scratch_shapes=[
            pltpu.VMEM((10, 4, 80, SLOTS), F32),
            pltpu.VMEM((TILES, SLOTS, SLOTS), F32),
            pltpu.VMEM((7, 4, SLOTS, SLOTS), F32),
            pltpu.VMEM((2, SLOTS, SLOTS), F32),
            pltpu.VMEM((4, FIELDS, BLOCKS, 8, SLOTS), F32),
            pltpu.VMEM((4, 2, BLOCKS, 8, SLOTS), F32),
            pltpu.VMEM((2, 2, SLOTS, SLOTS), F32),
            pltpu.VMEM((2, 2, CELLS + 2 * PAD, 8, SLOTS), F32),
            pltpu.VMEM((4, 2, 8, SLOTS), F32),
            pltpu.VMEM((6, 16, SLOTS), F32),
            pltpu.VMEM((4, 6, 8, SLOTS), F32),
            pltpu.VMEM((2, 6, 8, SLOTS), F32),
            pltpu.VMEM((2, 6, 8, SLOTS), F32),
            pltpu.SemaphoreType.DMA((1,)),
            pltpu.SemaphoreType.DMA((6, 8)),
            pltpu.SemaphoreType.DMA((6, 8)),
        ],
        compiler_params=pltpu.CompilerParams(
            collective_id=0, has_side_effects=True, vmem_limit_bytes=67_000_000
        ),
    )(
        base,
        edges,
        leaving_slot.reshape(8, SLOTS),
        jnp.broadcast_to(leaving_count, (8, SLOTS)),
        jnp.broadcast_to(leaving_side, (8, SLOTS)),
    )
    return (*results[:5], results[5].reshape(2, 6, 8, 1, SLOTS))


def solution(mesh):
    return jax.shard_map(
        functools.partial(per_device, mesh.shape["col"], mesh.shape["slab"]),
        mesh=mesh,
        in_specs=(
            P(None, "col", "slab", None),
            P(None, "col", "slab", None),
            P("col", "slab", None),
            P("col", "slab", None),
            P("col", "slab"),
            P("col", "slab", None),
            P("col", "slab"),
            P("col", "slab"),
        ),
        out_specs=(
            P("col", "slab", None),
            P("col", "slab", None),
            P(None, "col", "slab", None),
            P(None, "col", "slab", None),
            P(None, "col", "slab", None),
            P(None, None, "col", "slab", None),
        ),
        check_vma=False,
    )
```

time: 524 us -> 164 us (0.31)
  other arithmetic: 329 us -> 1.63 us
  Pallas kernels: 0 us -> 153 us
  starting transfers between devices: 113 us -> 0 us
  waiting for transfers between devices: 37.8 us -> 0 us
  loops' own time: 20 us -> 0 us
  local copies, waits for them, and re-layouts: 20.8 us -> 8.23 us
    reduce_sum x24 -> x0, other arithmetic: 322 us -> none  [the longest x6 89.8 us: density_terms(): jnp.sum(masses * kernel, -1)]
    pallas_call x0 -> x1, Pallas kernels: none -> 153 us  [per_device(): pl.pallas_call(functools.partial(kernel, n_col=n_col, n_slab=n_slab), out...]
    ppermute x26 -> x0, starting transfers between devices: 113 us -> none  [the longest x12 64.6 us: with_halo(): before = lax.ppermute(last, axis, up)]
    ppermute x26 -> x0, waiting for transfers between devices: 37.8 us -> none  [the longest x12 31.4 us: with_halo(): before = lax.ppermute(last, axis, up)]
    another operation x5 -> x0, loops' own time: 20 us -> none  [sweep(): totals = lax.map(one_column, jnp.arange(columns, dtype=jnp.int32))]
    gather x1 -> x0, local copies, waits for them, and re-layouts: 6.19 us -> none  [per_device(): state[:, leaving_slot.reshape(-1)].reshape(6, block_rows, 1, slot_count)]
    unnamed x23 -> x28, local copies, waits for them, and re-layouts: 0.73 us -> 6.89 us
    dynamic_slice x10 -> x0, local copies, waits for them, and re-layouts: 5.86 us -> none  [sweep(): totals = lax.map(one_column, jnp.arange(columns, dtype=jnp.int32))]
  transfers between devices with their start and end apart: 26 -> 0, of which waited for: 11 -> 0; matrix products, arithmetic and copies ran while one was open for 0% -> 0% of each run, Pallas kernels for 0% -> 0%
where the time goes in v1:
time: 164 us; the launch traced here: 163 us
  Pallas kernels  153 us (93%)
  local copies, waits for them, and re-layouts  8.23 us (5%)
    pallas_call x1, Pallas kernels, per_device(): pl.pallas_call(functools.partial(kernel, n_col=n_col, n_slab=n_slab), out...  153 us
    unnamed x28, local copies, waits for them, and re-layouts  6.89 us

profile of v1, /device:TPU:7, one launch (start us, length us, event | category | flops | bytes accessed | tf_op | source)
XLA Modules:
  0.0 163.4 jit_solution(6189915604266921899)
XLA Ops:
  0.6 0.0 copy-start.9
  0.6 0.6 copy-done.9
  1.3 0.0 copy-start.10
  1.3 0.7 broadcast_in_dim.31.leaving_count
  2.0 0.0 copy-done.10
  2.0 0.0 copy-start.8
  2.0 0.7 broadcast_in_dim.33.leaving_side
  2.6 0.0 copy-done.8
  2.6 0.0 copy-start.4
  2.6 0.0 copy-start.5
  2.6 1.0 select_bitcast_fusion.1
  3.6 0.0 copy-done.4
  3.6 0.0 copy-done.5
  3.7 0.0 copy-start
  3.7 0.7 copy-done
  4.5 0.6 select_maximum_fusion.edges
  5.1 152.8 %shard_map.127 = (f32[2,64,128]{2,1,0:T(8,128)}, f32[2,64,128]{2,1,0:T(8,128)}, f32[2,2,64,128]{3,2,1,0:T(8,128)}, f32[2,2,64,128]{3,2,1,0:T(8,128)}, f32[2,2,64...) custom-call(f32[6,2,64,128]{3,2,1,0:T(8,128)} %copy-done, f32[2,16,128]{2,1,0:T(8,128)} %select_maximum_fusion.edges, ...), custom_call_target="tpu_custom_call" | custom-call | tf_op jit(solution)/shard_map/pallas_call | solution.py:549
  157.9 0.0 copy-start.6
  157.9 0.0 copy-start.3
  157.9 1.5 copy.24
  159.4 0.0 copy-done.6
  159.4 0.6 copy.25
  160.1 0.0 copy-done.3
  160.1 0.0 copy-start.2
  160.1 0.7 copy.26
  160.7 0.3 copy-done.2
  161.0 0.0 copy-start.1
  161.0 0.7 copy.27
  161.7 0.3 copy-done.1
  162.0 0.7 copy.28
  162.6 0.1 copy-done.7
  162.8 0.6 copy.29
  (5 shorter events, 0.0 us)
Async XLA Ops:
  0.6 0.7 copy-start.9
  1.3 0.7 copy-start.10
  2.0 0.7 copy-start.8
  2.6 1.0 copy-start.4
  2.6 1.0 copy-start.5
  3.7 0.7 copy-start
  157.9 1.5 copy-start.6
  157.9 2.2 %copy-start.3 = (f32[2,2,64,128]{3,2,1,0:T(8,128)S(1)}, f32[2,2,64,128]{3,2,1,0:T(8,128)}, u32[]{:S(2)}) copy-start(f32[2,2,64,128]{3,2,1,0:T(8,128)} %get-tuple-element.42) | copy-start | bytes 393220
  160.1 1.0 copy-start.2
  161.0 1.0 copy-start.1
  162.0 0.8 copy-start.7

commit v2 on v1

--- a/solution.py
+++ b/solution.py
@@ -2,6 +2,7 @@
 
 import jax
 import jax.numpy as jnp
+import numpy as np
 from jax import lax
 from jax.experimental import pallas as pl
 from jax.experimental.pallas import tpu as pltpu
@@ -36,15 +37,65 @@
     (2, -1, ((2, 1, True, False),)),
     (1, CELLS, ((2, -1, True, False),)),
 )
-OWN0, OWN1, EXTRA0, HALO0, HALO1 = 0, 320, 448, 452, 650
-TILES = 848
+OWN0, OWN1, HALO0, HALO1 = 0, 320, 448, 646
+TILES = 844
+EXTRA_AT = (HALO0 + 1, HALO1 + 1, HALO1 + 2)
 PAD = 2
-FIELDS = 5
+FIELDS = 2
+PARTS = 24
+
+ONE = 21
+SIX = ((0, 0), (0, 1), (1, 0), (1, 1), (0, 2), (2, 0))
+FOUR = ((0, 0), (0, 1), (1, 0), (1, 1))
+HALF = 32
+
+
+def density_pairs(sx, sz):
+    x, z, vx, vz, u, e = 0, 3, 6, 9, 12, 15
+    near = [(ONE, ONE, 1 - sx * sx - sz * sz)]
+    approach = []
+    for a in range(3):
+        near += [(u + a, ONE, 1), (ONE, u + a, 1)]
+        approach += [(e + a, ONE, 1), (ONE, e + a, 1)]
+    for f, v, s in ((x, vx, sx), (z, vz, sz)):
+        near += [(f + a, f + b, 2) for a, b in SIX]
+        approach += [(v + a, f + b, -1) for a, b in FOUR] + [(f + a, v + b, -1) for a, b in FOUR]
+        for a in range(3):
+            near += [(f + a, ONE, 2 * s), (ONE, f + a, -2 * s)]
+        for a in range(2):
+            approach += [(v + a, ONE, -s), (ONE, v + a, s)]
+    return near, approach
+
+
+def force_pairs(sx, sz):
+    halves = []
+    for f, g, s in ((0, 9, sx), (3, 12, sz)):
+        half = [(f + a, 6 + b, 1) for a, b in SIX] + [(6 + a, f + b, 1) for a, b in SIX]
+        for a in range(3):
+            half += [(ONE, g + a, -1), (g + a, ONE, -1), (ONE, 6 + a, -s), (6 + a, ONE, s)]
+        halves.append(half)
+    return halves
+
+
+def form_matrices():
+    mine = np.zeros((2, PARTS, 2 * SLOTS), np.float32)
+    others = np.zeros((2, 9, 2 * HALF, PARTS), np.float32)
+    for form, (pairs, spread) in enumerate(((density_pairs, 18), (force_pairs, 15))):
+        mine[form, spread : spread + 3, SLOTS:] = 1.0
+        for sx in (-1, 0, 1):
+            for sz in (-1, 0, 1):
+                for half, terms in enumerate(pairs(sx, sz)):
+                    for i, (a, b, factor) in enumerate(terms):
+                        at = i + half * HALF
+                        mine[form, a, at] = 1.0
+                        others[form, (sx + 1) * 3 + sz + 1, at, b] = factor
+    return jnp.asarray(mine, jnp.bfloat16), jnp.asarray(others, jnp.bfloat16)
 
 
 class Phase:
-    def __init__(self, outs, a_fields, b_rows, shared, b_factors, a_factors):
+    def __init__(self, outs, a_fields, b_rows, shared, b_factors=None, a_factors=None, form=None):
         self.outs = outs
+        self.form = form
         self.a_fields = a_fields
         self.b_rows = b_rows
         self.shared = shared
@@ -58,6 +109,8 @@
     leaving_slot,
     leaving_count,
     leaving_side,
+    mine_matrix,
+    others_matrix,
     ratio_out,
     pressure_out,
     accel_out,
@@ -66,9 +119,12 @@
     arrived_out,
     rows,
     slopes,
-    columns,
+    cell_parts,
+    selectors,
     kept,
     lane_columns,
+    lane_terms,
+    tile_terms,
     lane_sums,
     column_sums,
     row_sums,
@@ -124,9 +180,17 @@
     for o in (0, 1):
         for c in (0, 1):
             column_sums[o, c] = jnp.zeros((SLOTS, SLOTS), F32)
-    for place in range(7):
+
+    def clear_parts(i, carry):
         for column in range(4):
-            columns[place, column] = jnp.zeros((SLOTS, SLOTS), F32)
+            cell_parts[column, pl.ds(pl.multiple_of(i * 8, 8), 8), :] = zeros
+        return carry
+
+    lax.fori_loop(0, 80 * PARTS // 8, clear_parts, 0)
+    part_of = lax.broadcasted_iota(jnp.int32, (PARTS, SLOTS), 0)
+    for i in range(FIELDS):
+        mine = (part_of >= 3 * i) & (part_of < 3 * i + 3)
+        selectors[:, i * SLOTS : (i + 1) * SLOTS] = jnp.where(mine, 1.0, 0.0).astype(jnp.bfloat16)
 
     barrier = pltpu.get_barrier_semaphore()
     for shift in around:
@@ -217,14 +281,68 @@
         for c in (0, 1):
             rows[field, 1 + c, FIRST : FIRST + CELLS, :] = value[c * CELLS : (c + 1) * CELLS]
 
-    def prepare(phase, column, k, place):
-        lane = jnp.full((8, SLOTS), k + FIRST, jnp.int32)
-        for b in range(BLOCKS):
-            for i, field in enumerate(phase.a_fields):
-                part = columns[field, column, b * 8 : b * 8 + 8, :]
-                lane_columns[place, i, b] = jnp.take_along_axis(part, lane, axis=1)
+    def prepare(phase, column, k, place, tiles):
+        fields = len(phase.a_fields)
+        at = pl.multiple_of((k + FIRST) * PARTS, PARTS)
+        parts = cell_parts[column, pl.ds(at, PARTS), :].astype(jnp.bfloat16)
+        if phase.form is not None:
+            spread = lax.dot_general(
+                parts, mine_matrix[phase.form], (((0,), (0,)), ((), ())), preferred_element_type=F32
+            )
+            lane_terms[place] = spread[:, :SLOTS].astype(jnp.bfloat16)
+            for i, (other, dk, _, _) in enumerate(tiles):
+                at = pl.multiple_of((k + (FIRST + dk)) * PARTS, PARTS)
+                parts = cell_parts[other, pl.ds(at, PARTS), :].astype(jnp.bfloat16)
+                matrix = others_matrix[phase.form, (other - column + 1) * 3 + dk + 1]
+                tile_terms[place, i] = jnp.dot(matrix, parts, preferred_element_type=F32).astype(jnp.bfloat16)
+            for b in range(BLOCKS):
+                lane_columns[place, 0, b] = spread[b * 8 : b * 8 + 8, SLOTS:]
+            return
+        spread = lax.dot_general(parts, selectors[:, 0 : fields * SLOTS], (((0,), (0,)), ((), ())), preferred_element_type=F32)
+        for i in range(fields):
+            for b in range(BLOCKS):
+                lane_columns[place, i, b] = spread[b * 8 : b * 8 + 8, i * SLOTS : (i + 1) * SLOTS]
+
+    def compute_form(phase, column, k, tiles, tile0, place):
+        outs = phase.outs
+        terms = lane_terms[place, :, : 2 * HALF]
+        blank = jnp.zeros((HALF, SLOTS), jnp.bfloat16)
+
+        def product_of(i):
+            left = jnp.concatenate([tile_terms[place, i, :HALF], blank], axis=0)
+            right = jnp.concatenate([blank, tile_terms[place, i, HALF:]], axis=0)
+            return jnp.dot(terms, jnp.concatenate([left, right], axis=1), preferred_element_type=F32)
+
+        following = product_of(0)
+        for i, (other, dk, give, take) in enumerate(tiles):
+            product = following
+            if i + 1 < len(tiles):
+                following = product_of(i + 1)
+            if take:
+                b_factor = jnp.broadcast_to(
+                    rows[phase.b_rows, other, pl.ds(k + (FIRST + dk), 1), :], (8, SLOTS)
+                )
+            given = [[None, None] for _ in range(outs)]
+            for b in range(BLOCKS):
+                block = slice(b * 8, b * 8 + 8)
+                shared = phase.shared(product[block, :SLOTS], product[block, SLOTS:], (tile0 + i, block))
+                for o in range(outs):
+                    if take:
+                        term = shared[o] * b_factor
+                        lane_sums[place, o, b] = term if i == 0 else lane_sums[place, o, b] + term
+                    if give:
+                        term = shared[o] * lane_columns[place, 0, b]
+                        so_far = given[o][b % 2]
+                        given[o][b % 2] = term if so_far is None else so_far + term
+            if give:
+                for o in range(outs):
+                    at = (o, other - 1, k + (PAD + dk))
+                    row_sums[at] = row_sums[at] + (given[o][0] + given[o][1])
 
     def compute(phase, column, k, tiles, tile0, place):
+        if phase.form is not None:
+            compute_form(phase, column, k, tiles, tile0, place)
+            return
         outs = phase.outs
         b_rows, theirs = [], []
         for other, dk, _, _ in tiles:
@@ -276,8 +394,8 @@
         transpose((1, 2))
 
         def prepare_own(k, parity):
-            prepare(phase, 1, k, 2 * parity)
-            prepare(phase, 2, k, 2 * parity + 1)
+            prepare(phase, 1, k, 2 * parity, OWN_TILES[0])
+            prepare(phase, 2, k, 2 * parity + 1, OWN_TILES[1])
 
         def compute_own(k, parity):
             compute(phase, 1, k, OWN_TILES[0], OWN0 + 5 * k, 2 * parity)
@@ -290,13 +408,15 @@
         def own(i, carry):
             for parity in (0, 1):
                 k = 1 + 2 * i + parity
-                prepare_own(k + 1, 1 - parity)
-                collect_own(k - 1, 1 - parity)
+                collect_own(k - 2, parity)
                 compute_own(k, parity)
+                prepare_own(k + 2, parity)
             return carry
 
         prepare_own(1, 0)
+        prepare_own(2, 1)
         lax.fori_loop(0, (CELLS - 2) // 2, own, 0)
+        collect_own(CELLS - 3, 0)
         collect_own(CELLS - 2, 1)
 
         receive(step, range(8))
@@ -310,27 +430,25 @@
             return carry
 
         lax.fori_loop(0, 2, ends, 0)
-        for i, (column, k, _) in enumerate(EXTRA):
-            prepare(phase, column, k, i)
-        tile0 = EXTRA0
-        for i, (column, k, tiles) in enumerate(EXTRA):
-            compute(phase, column, k, tiles, tile0, i)
-            tile0 += len(tiles)
-
         def prepare_halo(k, parity):
-            prepare(phase, 0, k, 2 * parity)
-            prepare(phase, 3, k, 2 * parity + 1)
+            prepare(phase, 0, k, 2 * parity, HALO_TILES[0])
+            prepare(phase, 3, k, 2 * parity + 1, HALO_TILES[1])
 
         def halo(i, carry):
             for parity in (0, 1):
                 k = 2 * i + parity - 1
-                prepare_halo(k + 1, 1 - parity)
                 compute(phase, 0, k, HALO_TILES[0], HALO0 + 3 * (k + 1), 2 * parity)
                 compute(phase, 3, k, HALO_TILES[1], HALO1 + 3 * (k + 1), 2 * parity + 1)
+                prepare_halo(k + 2, parity)
             return carry
 
         prepare_halo(-1, 0)
+        prepare_halo(0, 1)
         lax.fori_loop(0, (CELLS + 2) // 2, halo, 0)
+        for i, (column, k, tiles) in enumerate(EXTRA):
+            prepare(phase, column, k, i, tiles)
+        for i, (column, k, tiles) in enumerate(EXTRA):
+            compute(phase, column, k, tiles, EXTRA_AT[i], i)
 
     def sums(o):
         parts = []
@@ -339,34 +457,31 @@
             parts.append(by_row + column_sums[o, c].T[FIRST : FIRST + CELLS])
         return jnp.concatenate(parts, axis=0)
 
-    def transpose_of(pairs):
+    def spread_of(values):
         def of(which):
             for column in which:
-                for place, value in pairs:
-                    columns[place, column, :, 0:80] = value(column).T
+                for i, rest in enumerate(values(column)):
+                    for part in range(3):
+                        held = rest.astype(jnp.bfloat16).astype(F32)
+                        cell_parts[column, pl.ds(3 * i + part, 80, stride=PARTS), :] = held
+                        rest = rest - held
+                cell_parts[column, pl.ds(ONE, 80, stride=PARTS), :] = jnp.ones((80, SLOTS), F32)
 
         return of
 
-    def field(f):
-        return lambda column: rows[f, column]
-
-    def product(f):
-        return lambda column: rows[WEIGHT, column] * rows[f, column]
-
-    def geometry_rows(row, shift_x, shift_z):
-        return row(X) + shift_x, row(Z) + shift_z
-
-    def density_rows(row, shift_x, shift_z):
-        return (*geometry_rows(row, shift_x, shift_z), row(VX), row(VZ), row(MASS))
-
-    def density_shared(a, b, at):
-        dx = a[0] - b[0]
-        dz = a[1] - b[1]
-        support = jnp.maximum(1.0 - (dx * dx + dz * dz), 0.0)
+    def density_shared(near, approach, at):
+        support = jnp.maximum(near, 0.0)
         square = support * support
         slopes[at] = square
-        approach = (a[2] - b[2]) * dx + (a[3] - b[3]) * dz
         return square * support, square * approach
+
+    def density_values(column):
+        x, z, vx, vz = (rows[f, column] for f in (X, Z, VX, VZ))
+        return x, z, vx, vz, -(x * x + z * z), vx * x + vz * z, rows[MASS, column]
+
+    def force_values(column):
+        x, z, pressure = (rows[f, column] for f in (X, Z, P3))
+        return x, z, pressure, pressure * x, pressure * z, rows[WEIGHT, column]
 
     def first_rows(row, shift_x, shift_z):
         weight = row(WEIGHT)
@@ -378,24 +493,16 @@
 
         return of
 
-    def force_rows(row, shift_x, shift_z):
-        return (*geometry_rows(row, shift_x, shift_z), row(WEIGHT), row(P3))
-
-    def force_shared(a, b, at):
-        lifted = slopes[at] * (b[3] - a[3])
-        return lifted * (a[0] - b[0]), lifted * (a[1] - b[1])
-
-    def repeat(part, times):
-        return lambda values: (values[part],) * times
-
-    CW, CQ, CP = 4, 5, 6
+    def force_shared(pull_x, pull_z, at):
+        square = slopes[at]
+        return square * pull_x, square * pull_z
 
     send(0)
     local.wait()
     run(
-        Phase(2, (0, 1, 2, 3, 4), density_rows, density_shared, repeat(4, 2), repeat(4, 2)),
+        Phase(2, (), MASS, density_shared, form=0),
         0,
-        transpose_of([(f, field(f)) for f in (X, Z, VX, VZ, MASS)]),
+        spread_of(density_values),
     )
     live_mass = own_rows(MASS)
     alive = live_mass > 0.0
@@ -413,24 +520,24 @@
         if sweep == 0:
             phase = Phase(
                 2,
-                (CW, CQ),
+                (0, 1),
                 first_rows,
                 lambda a, b, at: (slopes[at],) * 2,
                 lambda b: b,
                 lambda a: a,
             )
-            moved = [(CW, field(WEIGHT)), (CQ, product(P0))]
+            moved = lambda column: (rows[WEIGHT, column], rows[WEIGHT, column] * rows[P0, column])
         else:
             phase = Phase(
                 1,
-                (CQ,),
+                (0,),
                 next_rows(pressure_field),
                 lambda a, b, at: (slopes[at],),
                 lambda b: b,
                 lambda a: a,
             )
-            moved = [(CQ, product(pressure_field))]
-        run(phase, 1 + sweep, transpose_of(moved))
+            moved = lambda column, f=pressure_field: (rows[WEIGHT, column] * rows[f, column],)
+        run(phase, 1 + sweep, spread_of(moved))
         if sweep == 0:
             kept[1] = COMPRESSION + sums(0)
             pulled = sums(1)
@@ -443,9 +550,9 @@
     for c in (0, 1):
         pressure_out[c] = pressure[c * CELLS : (c + 1) * CELLS]
     run(
-        Phase(2, (X, Z, CW, CP), force_rows, force_shared, repeat(2, 2), repeat(2, 2)),
+        Phase(2, (), WEIGHT, force_shared, form=1),
         4,
-        transpose_of([(CP, field(P3))]),
+        spread_of(force_values),
     )
 
     live_mass = own_rows(MASS)
@@ -460,10 +567,10 @@
             accel_out[o, c] = accel[part]
             velocity_out[o, c] = velocity_new[part]
             offsets_out[o, c] = offsets_new[part]
-        columns[o, 0] = offsets_new.T
-        columns[2 + o, 0] = velocity_new.T
-    columns[4, 0] = own_rows(P3).T
-    columns[5, 0] = live_mass.T
+        slopes[o] = offsets_new.T
+        slopes[2 + o] = velocity_new.T
+    slopes[4] = own_rows(P3).T
+    slopes[5] = live_mass.T
 
     chosen = leaving_slot[...]
     cell = chosen // SLOTS
@@ -477,7 +584,7 @@
     for b in range(8):
         cell_is.append(jnp.where(sublanes == cell[b : b + 1], 1.0, 0.0).astype(jnp.bfloat16))
     for comp in range(6):
-        value = columns[comp, 0]
+        value = slopes[comp]
         high = value.astype(jnp.bfloat16)
         rest = value - high.astype(F32)
         middle = rest.astype(jnp.bfloat16)
@@ -549,14 +656,17 @@
     results = pl.pallas_call(
         functools.partial(kernel, n_col=n_col, n_slab=n_slab),
         out_shape=(shape(*cells), shape(*cells), shape(2, *cells), shape(2, *cells), shape(2, *cells), shape(2, 6, 8, SLOTS)),
-        in_specs=[anywhere, anywhere, vmem, vmem, vmem],
+        in_specs=[anywhere, anywhere, vmem, vmem, vmem, vmem, vmem],
         out_specs=[vmem] * 6,
         scratch_shapes=[
             pltpu.VMEM((10, 4, 80, SLOTS), F32),
             pltpu.VMEM((TILES, SLOTS, SLOTS), F32),
-            pltpu.VMEM((7, 4, SLOTS, SLOTS), F32),
+            pltpu.VMEM((4, 80 * PARTS, SLOTS), F32),
+            pltpu.VMEM((PARTS, FIELDS * SLOTS), jnp.bfloat16),
             pltpu.VMEM((2, SLOTS, SLOTS), F32),
             pltpu.VMEM((4, FIELDS, BLOCKS, 8, SLOTS), F32),
+            pltpu.VMEM((4, SLOTS, SLOTS), jnp.bfloat16),
+            pltpu.VMEM((4, 5, 2 * HALF, SLOTS), jnp.bfloat16),
             pltpu.VMEM((4, 2, BLOCKS, 8, SLOTS), F32),
             pltpu.VMEM((2, 2, SLOTS, SLOTS), F32),
             pltpu.VMEM((2, 2, CELLS + 2 * PAD, 8, SLOTS), F32),
@@ -578,6 +688,7 @@
         leaving_slot.reshape(8, SLOTS),
         jnp.broadcast_to(leaving_count, (8, SLOTS)),
         jnp.broadcast_to(leaving_side, (8, SLOTS)),
+        *form_matrices(),
     )
     return (*results[:5], results[5].reshape(2, 6, 8, 1, SLOTS))
 

time: 164 us -> 156 us (0.951)
  Pallas kernels: 153 us -> 145 us
    pallas_call x1, Pallas kernels: 153 us -> 145 us  [per_device(): pl.pallas_call(functools.partial(kernel, n_col=n_col, n_slab=n_slab), out...]
where the time goes in v2:
time: 156 us
  Pallas kernels  145 us (93%)
  local copies, waits for them, and re-layouts  8.23 us (5%)
  other arithmetic  1.63 us (1%)
    pallas_call x1, Pallas kernels, per_device(): pl.pallas_call(functools.partial(kernel, n_col=n_col, n_slab=n_slab), out...  145 us
    unnamed x28, local copies, waits for them, and re-layouts  6.89 us

profile of v2, /device:TPU:7, one launch (start us, length us, event | category | flops | bytes accessed | tf_op | source)
XLA Modules:
  0.0 155.7 jit_solution(11408356587824317091)
XLA Ops:
  0.6 0.0 copy-start.9
  0.6 0.6 copy-done.9
  1.3 0.0 copy-start.10
  1.3 0.7 broadcast_in_dim.31.leaving_count
  2.0 0.0 copy-done.10
  2.0 0.0 copy-start.8
  2.0 0.7 broadcast_in_dim.33.leaving_side
  2.6 0.0 copy-done.8
  2.6 0.0 copy-start.4
  2.6 0.0 copy-start.5
  2.6 1.0 select_bitcast_fusion.1
  3.6 0.0 copy-done.4
  3.6 0.0 copy-done.5
  3.7 0.0 copy-start
  3.7 0.7 copy-done
  4.5 0.6 select_maximum_fusion.edges
  5.1 145.2 %shard_map.145 = (f32[2,64,128]{2,1,0:T(8,128)}, f32[2,64,128]{2,1,0:T(8,128)}, f32[2,2,64,128]{3,2,1,0:T(8,128)}, f32[2,2,64,128]{3,2,1,0:T(8,128)}, f32[2,2,64...) custom-call(f32[6,2,64,128]{3,2,1,0:T(8,128)} %copy-done, f32[2,16,128]{2,1,0:T(8,128)} %select_maximum_fusion.edges, ...), custom_call_target="tpu_custom_call" | custom-call | tf_op jit(solution)/shard_map/pallas_call | solution.py:656
  150.2 0.0 copy-start.6
  150.3 0.0 copy-start.3
  150.3 1.5 copy.26
  151.8 0.0 copy-done.6
  151.8 0.6 copy.27
  152.4 0.0 copy-done.3
  152.4 0.0 copy-start.2
  152.4 0.7 copy.28
  153.1 0.3 copy-done.2
  153.4 0.7 copy.29
  154.0 0.3 copy-done.1
  154.3 0.0 copy-start.7
  154.3 0.7 copy.30
  155.0 0.1 copy-done.7
  155.1 0.6 copy.31
  (5 shorter events, 0.0 us)
Async XLA Ops:
  0.6 0.7 copy-start.9
  1.3 0.7 copy-start.10
  2.0 0.7 copy-start.8
  2.6 1.0 copy-start.4
  2.6 1.0 copy-start.5
  3.7 0.7 copy-start
  150.2 1.5 copy-start.6
  150.3 2.2 %copy-start.3 = (f32[2,2,64,128]{3,2,1,0:T(8,128)S(1)}, f32[2,2,64,128]{3,2,1,0:T(8,128)}, u32[]{:S(2)}) copy-start(f32[2,2,64,128]{3,2,1,0:T(8,128)} %get-tuple-element.42) | copy-start | bytes 393220
  152.4 1.0 copy-start.2
  153.4 1.0 copy-start.1
  154.3 0.8 copy-start.7

commit v3 on v2

--- a/solution.py
+++ b/solution.py
@@ -107,15 +107,12 @@
     base,
     edges,
     leaving_slot,
-    leaving_count,
-    leaving_side,
+    leaving_tags,
     mine_matrix,
     others_matrix,
-    ratio_out,
+    density_out,
     pressure_out,
     accel_out,
-    velocity_out,
-    offsets_out,
     arrived_out,
     rows,
     slopes,
@@ -200,7 +197,6 @@
             pl.semaphore_signal(barrier, inc=1, device_id=device(shift), device_id_type=MESH)
 
     peers = sum(jnp.where(there(shift), 1, 0).astype(jnp.int32) for shift in around)
-    pl.semaphore_wait(barrier, peers)
 
     def copy_of(step, n):
         shift = around[n]
@@ -383,7 +379,7 @@
                 at = (o, column - 1, slice(b * 8, b * 8 + 8), slice(None))
                 column_sums[at] = jnp.where(here, total, column_sums[at])
 
-    def run(phase, step, transpose):
+    def run(phase, step, transpose, early=None):
         def clear(i, carry):
             for o in range(phase.outs):
                 row_sums[o, 0, i] = zeros
@@ -415,7 +411,12 @@
 
         prepare_own(1, 0)
         prepare_own(2, 1)
-        lax.fori_loop(0, (CELLS - 2) // 2, own, 0)
+        begin = 0
+        if early is not None:
+            begin = 3
+            lax.fori_loop(0, begin, own, 0)
+            early()
+        lax.fori_loop(begin, (CELLS - 2) // 2, own, 0)
         collect_own(CELLS - 3, 0)
         collect_own(CELLS - 2, 1)
 
@@ -497,20 +498,23 @@
         square = slopes[at]
         return square * pull_x, square * pull_z
 
-    send(0)
+    def first_send():
+        pl.semaphore_wait(barrier, peers)
+        send(0)
+
     local.wait()
     run(
         Phase(2, (), MASS, density_shared, form=0),
         0,
         spread_of(density_values),
+        first_send,
     )
     live_mass = own_rows(MASS)
     alive = live_mass > 0.0
     density = jnp.where(alive, sums(0), 0.0)
     diverge = -6.0 * sums(1)
-    ratio = density / REST_DENSITY
     for c in (0, 1):
-        ratio_out[c] = ratio[c * CELLS : (c + 1) * CELLS]
+        density_out[c] = density[c * CELLS : (c + 1) * CELLS]
     weight = jnp.where(alive, 6.0 * live_mass / jnp.where(alive, density, 1.0), 0.0)
     set_own(WEIGHT, weight)
     send(1)
@@ -565,8 +569,6 @@
         for c in (0, 1):
             part = slice(c * CELLS, (c + 1) * CELLS)
             accel_out[o, c] = accel[part]
-            velocity_out[o, c] = velocity_new[part]
-            offsets_out[o, c] = offsets_new[part]
         slopes[o] = offsets_new.T
         slopes[2 + o] = velocity_new.T
     slopes[4] = own_rows(P3).T
@@ -576,26 +578,27 @@
     cell = chosen // SLOTS
     slot = chosen - cell * SLOTS
     lanes = lax.broadcasted_iota(jnp.int32, (8, SLOTS), 1)
-    filled = lanes < leaving_count[...]
-    upward = filled & (leaving_side[...] == 1)
-    downward = filled & (leaving_side[...] == 0)
+    filled = lanes < leaving_tags[0]
+    upward = filled & (leaving_tags[1] == 1)
+    downward = filled & (leaving_tags[1] == 0)
     sublanes = lax.broadcasted_iota(jnp.int32, (SLOTS, SLOTS), 0)
-    cell_is, slot_is = [], []
-    for b in range(8):
-        cell_is.append(jnp.where(sublanes == cell[b : b + 1], 1.0, 0.0).astype(jnp.bfloat16))
+    cell_is = []
+    for b in range(0, 8, 2):
+        pair = [jnp.where(sublanes == cell[i : i + 1], 1.0, 0.0).astype(jnp.bfloat16) for i in (b, b + 1)]
+        cell_is.append(jnp.concatenate([jnp.concatenate(pair, axis=1)] * 3, axis=0))
     for comp in range(6):
-        value = slopes[comp]
-        high = value.astype(jnp.bfloat16)
-        rest = value - high.astype(F32)
-        middle = rest.astype(jnp.bfloat16)
-        low = (rest - middle.astype(F32)).astype(jnp.bfloat16)
+        rest = slopes[comp]
+        parts = []
+        for _ in range(3):
+            parts.append(rest.astype(jnp.bfloat16))
+            rest = rest - parts[-1].astype(F32)
+        parts = jnp.concatenate(parts, axis=1)
         picked = []
-        for b in range(8):
-            by_slot = sum(
-                jnp.dot(part, cell_is[b], preferred_element_type=F32) for part in (low, middle, high)
-            )
-            one = jnp.where(sublanes == slot[b : b + 1], by_slot, 0.0)
-            picked.append(jnp.sum(one, axis=0, keepdims=True))
+        for b in range(0, 8, 2):
+            by_slot = jnp.dot(parts, cell_is[b // 2], preferred_element_type=F32)
+            for i in (0, 1):
+                one = jnp.where(sublanes == slot[b + i : b + i + 1], by_slot[:, i * SLOTS : (i + 1) * SLOTS], 0.0)
+                picked.append(jnp.sum(one, axis=0, keepdims=True))
         block = jnp.concatenate(picked, axis=0)
         block_send[0, comp] = jnp.where(downward, block, 0.0)
         block_send[1, comp] = jnp.where(upward, block, 0.0)
@@ -655,9 +658,9 @@
     shape = lambda *s: jax.ShapeDtypeStruct(s, F32)
     results = pl.pallas_call(
         functools.partial(kernel, n_col=n_col, n_slab=n_slab),
-        out_shape=(shape(*cells), shape(*cells), shape(2, *cells), shape(2, *cells), shape(2, *cells), shape(2, 6, 8, SLOTS)),
-        in_specs=[anywhere, anywhere, vmem, vmem, vmem, vmem, vmem],
-        out_specs=[vmem] * 6,
+        out_shape=(shape(*cells), shape(*cells), shape(2, *cells), shape(2, 6, 8, SLOTS)),
+        in_specs=[anywhere, anywhere, vmem, vmem, vmem, vmem],
+        out_specs=[vmem] * 4,
         scratch_shapes=[
             pltpu.VMEM((10, 4, 80, SLOTS), F32),
             pltpu.VMEM((TILES, SLOTS, SLOTS), F32),
@@ -686,11 +689,22 @@
         base,
         edges,
         leaving_slot.reshape(8, SLOTS),
-        jnp.broadcast_to(leaving_count, (8, SLOTS)),
-        jnp.broadcast_to(leaving_side, (8, SLOTS)),
+        jnp.broadcast_to(jnp.stack([leaving_count, leaving_side]), (2, 8, SLOTS)),
         *form_matrices(),
     )
-    return (*results[:5], results[5].reshape(2, 6, 8, 1, SLOTS))
+    density, pressure, pull, arrived = results
+    pulled = pull - jnp.array([0.0, GRAVITY], F32)[:, None, None, None]
+    alive = jnp.arange(SLOTS, dtype=jnp.int32)[None, None, :] < lax.optimization_barrier(counts)[:, :, None]
+    velocity_new = jnp.where(alive[None], velocity + TIME_STEP * pulled, 0.0)
+    offsets_new = jnp.where(alive[None], offsets + TIME_STEP * velocity_new, 0.0)
+    return (
+        density / REST_DENSITY,
+        jnp.where(alive, pressure, 0.0),
+        jnp.where(alive[None], pull, 0.0),
+        velocity_new,
+        offsets_new,
+        arrived.reshape(2, 6, 8, 1, SLOTS),
+    )
 
 
 def solution(mesh):

time: 156 us -> 151 us (0.968)
  local copies, waits for them, and re-layouts: 8.23 us -> 3.41 us
  other arithmetic: 1.63 us -> 5.07 us
  Pallas kernels: 145 us -> 142 us
    unnamed x28 -> x19, local copies, waits for them, and re-layouts: 6.89 us -> 2.72 us
    pallas_call x1, Pallas kernels: 145 us -> 142 us  [per_device(): pl.pallas_call(functools.partial(kernel, n_col=n_col, n_slab=n_slab), out...]
    select_n x0 -> x1, other arithmetic: none -> 1.7 us  [per_device(): jnp.where(alive[None], offsets + TIME_STEP * velocity_new, 0.0)]
    div x0 -> x1, other arithmetic: none -> 1.63 us  [per_device(): density / REST_DENSITY]
where the time goes in v3:
time: 151 us
  Pallas kernels  142 us (94%)
  other arithmetic  5.07 us (3%)
  local copies, waits for them, and re-layouts  3.41 us (2%)
    pallas_call x1, Pallas kernels, per_device(): pl.pallas_call(functools.partial(kernel, n_col=n_col, n_slab=n_slab), out...  142 us

profile of v3, /device:TPU:7, one launch (start us, length us, event | category | flops | bytes accessed | tf_op | source)
XLA Modules:
  0.0 151.3 jit_solution(4045932955201716713)
XLA Ops:
  0.6 0.0 copy-start.3
  0.6 0.0 copy-start.1
  0.7 1.0 select_bitcast_fusion.1
  1.7 0.0 copy-done.3
  1.7 0.0 copy-done.1
  1.7 0.0 copy-start
  1.7 0.7 copy-done
  2.5 0.6 select_maximum_fusion.edges
  3.1 0.0 copy-start.7
  3.1 0.0 copy-start.8
  3.1 0.7 copy-done.7
  3.8 0.0 copy-done.8
  3.8 0.7 broadcast_in_dim.51.leaving_tags
  4.5 142.1 %shard_map.154 = (f32[2,64,128]{2,1,0:T(8,128)}, f32[2,64,128]{2,1,0:T(8,128)}, f32[2,2,64,128]{3,2,1,0:T(8,128)}, f32[2,6,8,128]{3,2,1,0:T(8,128)}) custom-call(f32[6,2,64,128]{3,2,1,0:T(8,128)} %copy-done, f32[2,16,128]{2,1,0:T(8,128)} %select_maximum_fusion.edges, s32[8,128]{1,0:T(8,128)} %bitcast.16, s32[2,8,128]{2,1,0:T(8,128)} %broadcast_in_dim.51.leaving_tags, ...), custom_call_target="tpu_custom_call" | custom-call | tf_op jit(solution)/shard_map/pallas_call | solution.py:659
  146.5 0.0 copy-start.6
  146.5 0.7 copy-done.6
  147.2 0.0 copy-start.2
  147.2 0.0 copy-start.4
  147.2 1.6 %broadcast_multiply_fusion = (f32[2,64,128]{2,1,0:T(8,128)}, f32[2,64,128]{2,1,0:T(8,128)}) fusion(f32[2,64,128]{2,1,0:T(8,128)} %get-tuple-element.10, f32[2,64,128]{2,1,0:T(8,128)} %get-tuple-element.11, s32[2,64]{1,0:T(2,128)S(1)} %copy-done.6), kind=kLoop, calls=%fused_computation.11 | loop fusion | flops 49152 | bytes 262656 | tf_op jit(solution)/shard_map/div | solution.py:701
  148.8 0.1 iota_compare_fusion
  148.9 0.0 copy-done.2
  148.9 0.0 copy-done.4
  149.0 0.0 copy-start.5
  149.0 1.7 %add_select_fusion = (f32[2,2,64,128]{3,2,1,0:T(8,128)}, f32[2,2,64,128]{3,2,1,0:T(8,128)}, f32[2,2,64,128]{3,2,1,0:T(8,128)}) fusion(f32[2,2,64,128]{3,2,1,0:T(8,128)S(1)} %copy-done.4, pred[2,64,128]{2,1,0:T(8,128)(4,1)S(1)} %iota_compare_fusion, f32[2,2,64,128]{3,2,1,0:T(8,128)S(1)} %copy-done.2, f32[2,2,64,128]{3,2,1,0:T(8,128)} %get-tuple-element.12), kind=kLoop, calls=%fused_computation.5 | loop fusion | flops 262144 | bytes 802816 | tf_op jit(solution)/shard_map/jit(_where)/select_n | solution.py:699
  150.7 0.0 copy-done.5
  150.7 0.6 copy.22
  (5 shorter events, 0.0 us)
Async XLA Ops:
  0.6 1.0 copy-start.3
  0.6 1.0 copy-start.1
  1.7 0.7 copy-start
  3.1 0.7 copy-start.7
  3.1 0.7 copy-start.8
  146.5 0.7 copy-start.6
  147.2 1.7 %copy-start.2 = (f32[2,2,64,128]{3,2,1,0:T(8,128)S(1)}, f32[2,2,64,128]{3,2,1,0:T(8,128)}, u32[]{:S(2)}) copy-start(f32[2,2,64,128]{3,2,1,0:T(8,128)} %param.12) | copy-start | bytes 393220
  147.2 1.7 %copy-start.4 = (f32[2,2,64,128]{3,2,1,0:T(8,128)S(1)}, f32[2,2,64,128]{3,2,1,0:T(8,128)}, u32[]{:S(2)}) copy-start(f32[2,2,64,128]{3,2,1,0:T(8,128)} %param.11) | copy-start | bytes 393220
  149.0 1.7 %copy-start.5 = (f32[2,6,8,128]{3,2,1,0:T(8,128)S(1)}, f32[2,6,8,128]{3,2,1,0:T(8,128)}, u32[]{:S(2)}) copy-start(f32[2,6,8,128]{3,2,1,0:T(8,128)} %get-tuple-element.13) | copy-start | bytes 147460
